TPU v7x, 512 devices: a whole 4x4x16 slice. The times are simulated.
512 devices in a mesh: grp: 16 (over y, x), tile: 32 (over z, core).
Axes of the slice: x: 4, y: 4, z: 16, core: 2. Of those that a mesh axis runs over, the one named last changes fastest.
Arguments:
- features: bfloat16 [131072, 128], P(('grp', 'tile')), may hold values from -6 to 6
- source_rows: int32 [27, 1024, 128], P(None, ('grp', 'tile')), may hold values from -1 to 127, as said below
- target_codes: int32 [27, 1024], P(None, ('grp', 'tile')), may hold values from 0 to 5, as said below
- block_count: int32 [512], P(('grp', 'tile')), may hold values from 1 to 2, as said below
- weight_one: bfloat16 [27, 128, 128], replicated, may hold values from -0.125 to 0.125
- weight_two: bfloat16 [27, 128, 128], replicated, may hold values from -0.125 to 0.125
- out_cotangent: bfloat16 [131072, 128], P(('grp', 'tile')), may hold values from -6 to 6
Outputs:
- block_out: bfloat16 [131072, 128], P(('grp', 'tile'))
- input_grad: bfloat16 [131072, 128], P(('grp', 'tile'))
- wgrad_one: float32 [3456, 128], P('grp')
- wgrad_two: float32 [3456, 128], P('grp')
Inputs may be any that keep to these rules, and one draw needn't show every extreme that they name: `source_rows`: entry [k, j, r] is the row of source block j that reaches row r of its target block under offset k, or -1 for none. `target_codes`: a code s * 2 + b names block b of tile t - 1 + s of the same group, t being the source block's tile; offset k = 9 (dx + 1) + 3 (dy + 1) + (dz + 1); s = 1 except s = 0 for offsets with dz = -1 from block 0 of a tile, and s = 2 for offsets with dz = +1 from the last active block of a tile. Blocks of a tile from block_count on are empty.
All inputs are finite; a program needn't handle non-finite values.
Results may differ from a plain program's by a relative error of at most 0.025.
Values may be sent and summed in bfloat16 or wider, within the bound.
A program may use at most 64 MiB of HBM per device.

v0:
```python
import jax
import jax.numpy as jnp
from jax import lax
from jax.sharding import PartitionSpec as P


def padded_2(cells, sides, width):
    for axis, dim in sides:
        count = lax.axis_size(axis)
        ends = count - 1
        head = lax.slice_in_dim(cells, 0, width, axis=dim)
        tail = lax.slice_in_dim(cells, cells.shape[dim] - width, cells.shape[dim], axis=dim)
        cells = jnp.concatenate(
            [
                lax.ppermute(tail, axis, [(i, (i + 1) % count) for i in range(ends)]),
                cells,
                lax.ppermute(head, axis, [((i + 1) % count, i) for i in range(ends)]),
            ],
            axis=dim,
        )
    return cells


def split_up(value, dim, count):
    before, after = (value.shape[:dim], value.shape[dim + 1 :])
    return jnp.moveaxis(value.reshape(*before, count, -1, *after), dim, 0)


def sent_and_summed(value, axis, dim):
    pieces = split_up(value, dim, lax.axis_size(axis))
    arrived = lax.all_to_all(pieces, axis, split_axis=0, concat_axis=0, tiled=True)
    return arrived.astype(jnp.float32).sum(axis=0)


def laid_out(pieces, dim):
    pieces = jnp.moveaxis(pieces, 0, dim)
    dims = pieces.shape
    return pieces.reshape(*dims[:dim], dims[dim] * dims[dim + 1], *dims[dim + 2 :])


def from_everyone(value, axis):
    count = lax.axis_size(axis)
    return lax.all_to_all(
        jnp.broadcast_to(value[None], (count, *value.shape)), axis, 0, 0, tiled=True
    )


def collect(value, axis, dim):
    return laid_out(from_everyone(value, axis), dim)


def silu_grad(values):
    sigma = jax.nn.sigmoid(values)
    return sigma * (1.0 + values * (1.0 - sigma))


def gather_rows(field, selector):
    offsets, blocks_dev, block_rows, _ = selector.shape
    blocked = field.reshape(blocks_dev, block_rows, field.shape[1])
    picked = jnp.einsum("kbrs,bsc->kbrc", selector, blocked, preferred_element_type=jnp.float32)
    return picked.astype(jnp.bfloat16).reshape(offsets, blocks_dev * block_rows, field.shape[1])


def spread_terms(picked, weights, codes):
    offsets, total_rows, channels = picked.shape
    blocks_dev = codes.shape[1]
    block_rows = total_rows // blocks_dev
    partial_value = jnp.einsum("kmc,kcd->kmd", picked, weights, preferred_element_type=jnp.float32)
    one_hot = (
        codes[:, :, None] == jnp.arange(3 * blocks_dev, dtype=jnp.int32)[None, None, :]
    ).astype(jnp.float32)
    buffer = jnp.einsum(
        "kis,kirc->src",
        one_hot,
        partial_value.reshape(offsets, blocks_dev, block_rows, -1),
        precision=lax.Precision.HIGHEST,
    )
    return buffer.reshape(3, blocks_dev * block_rows, -1)


def join_partials(buffer):
    span = buffer.shape[1]
    padded = padded_2(jnp.concatenate([buffer[0], buffer[2]], axis=0), (("tile", 0),), span)
    return buffer[1] + padded[:span] + padded[3 * span :]


def neighbor_rows(grads):
    span = grads.shape[0]
    return padded_2(grads, (("tile", 0),), span)


def pull_back(stacked, codes, picked, selector_wide, weights):
    offsets, total_rows, channels = picked.shape
    blocks_dev = codes.shape[1]
    block_rows = total_rows // blocks_dev
    grid_blocks = stacked.reshape(3 * blocks_dev, block_rows, -1)
    grad_rows = jnp.take(grid_blocks, codes.reshape(-1), axis=0).reshape(offsets, total_rows, -1)
    wgrad = jnp.einsum("kmc,kmd->kcd", picked, grad_rows, preferred_element_type=jnp.float32)
    grad_pick = jnp.einsum("kmd,kcd->kmc", grad_rows, weights, preferred_element_type=jnp.float32)
    grad_pick = grad_pick.reshape(offsets, blocks_dev, block_rows, channels)
    grad_in = jnp.einsum(
        "kbrs,kbrc->bsc", selector_wide, grad_pick, precision=lax.Precision.HIGHEST
    )
    return (wgrad, grad_in.reshape(total_rows, channels))


def on_device(
    features, source_rows, target_codes, block_count, weight_one, weight_two, out_cotangent
):
    offsets, blocks_dev, block_rows = source_rows.shape
    channels = features.shape[1]
    active = jnp.arange(blocks_dev, dtype=jnp.int32) < block_count[0]
    row_mask = jnp.repeat(active, block_rows).astype(jnp.float32)[:, None]
    valid_rows = (source_rows >= 0) & active[None, :, None]
    matches = (
        source_rows[:, :, :, None] == jnp.arange(block_rows, dtype=jnp.int32)[None, None, None, :]
    ) & valid_rows[:, :, :, None]
    selector = matches.astype(jnp.bfloat16)
    selector_wide = matches.astype(jnp.float32)
    pick_in = gather_rows(features, selector)
    pre_one = join_partials(spread_terms(pick_in, weight_one, target_codes))
    hidden = (jax.nn.silu(pre_one) * row_mask).astype(jnp.bfloat16)
    pick_mid = gather_rows(hidden, selector)
    total = join_partials(spread_terms(pick_mid, weight_two, target_codes)) + features.astype(
        jnp.float32
    )
    result = (jax.nn.silu(total) * row_mask).astype(jnp.bfloat16)
    grad_sum = (out_cotangent.astype(jnp.float32) * silu_grad(total) * row_mask).astype(
        jnp.bfloat16
    )
    wgrad_two, grad_mid = pull_back(
        neighbor_rows(grad_sum), target_codes, pick_mid, selector_wide, weight_two
    )
    grad_pre = (grad_mid * silu_grad(pre_one) * row_mask).astype(jnp.bfloat16)
    wgrad_one, grad_conv = pull_back(
        neighbor_rows(grad_pre), target_codes, pick_in, selector_wide, weight_one
    )
    input_grad = (grad_conv + grad_sum.astype(jnp.float32)).astype(jnp.bfloat16)
    stacked = jnp.stack([wgrad_one, wgrad_two]).reshape(2, offsets * channels, channels)
    shard_part = sent_and_summed(stacked.astype(jnp.bfloat16), "grp", 1)
    flat_part = shard_part.reshape(-1)
    summed_piece = sent_and_summed(flat_part.astype(jnp.bfloat16), "tile", 0)
    collected = collect(summed_piece, "tile", 0)
    owned = collected.reshape(shard_part.shape)
    voxel_total = lax.axis_size("grp") * lax.axis_size("tile") * blocks_dev * block_rows
    scale = float(voxel_total) ** (-0.5)
    owned = owned * scale
    return (result, input_grad, owned[0], owned[1])


def solution(mesh):
    in_specs = (
        P(("grp", "tile"), None),
        P(None, ("grp", "tile"), None),
        P(None, ("grp", "tile")),
        P(("grp", "tile")),
        P(),
        P(),
        P(("grp", "tile"), None),
    )
    out_specs = (P(("grp", "tile"), None), P(("grp", "tile"), None), P("grp", None), P("grp", None))
    return jax.shard_map(
        on_device, mesh=mesh, in_specs=in_specs, out_specs=out_specs, check_vma=False
    )
```

profile of v0, /device:TPU:1, one launch (start us, length us, event | category | flops | bytes accessed | tf_op | source)
XLA Modules:
  0.0 171.5 jit_solution(2575235099103968838)
XLA Ops:
  1.4 0.8 copy.62
  2.1 0.8 compare_and_fusion
  3.0 1.9 %convert_bitcast_fusion.1 = bf16[27,2,128,128]{3,2,0,1:T(8,128)(2,1)S(1)} fusion(bf16[2,128,128,1]{2,1,3,0:T(8,128)(2,1)} %bitcast.117, s32[27,2,128]{2,0,1:T(8,128)S(1)} %copy.62, pred[27,2,128]{2,0,1:T(8,128)(4,1)S(1)} %copy.63), kind=kOutput, calls=%fused_computation.16 | convolution fusion | flops 229146624 | bytes 1869568 | tf_op jit(solution)/shard_map/kbrs,bsc->kbrc/dot_general | solution.py:60
  5.1 1.0 copy-done.5
  6.8 3.4 %fusion.27 = f32[6,128,128]{2,0,1:T(8,128)S(1)} fusion(f32[27,2,128,128]{3,2,1,0:T(8,128)S(1)} %bitcast.98, s32[27,2]{0,1:T(2,128)S(1)} %copy-done.14), kind=kOutput, calls=%fused_computation.29 | convolution fusion | flops 63701316 | bytes 3932376 | tf_op jit(solution)/shard_map/kis,kirc->src/dot_general | solution.py:72
  10.3 4.9 %collective-permute-start = (f32[256,128]{1,0:T(8,128)S(1)}, f32[256,128]{1,0:T(8,128)S(1)}, u32[]{:S(2)}, u32[]{:S(2)}) collective-permute-start(f32[256,128]{1,0:T(8,128)S(1)} %bitcast.112), channel_id=1, source_target_pairs={{0,1},{1,2},{2,3},{3,4},{4,5},{5,6},{6,7},{7,8},{8,9},{9,10},{10,1... | collective-permute-start | bytes 393224 | tf_op jit(solution)/shard_map/ppermute | solution.py:15
  15.3 5.1 %collective-permute-start.1 = (f32[256,128]{1,0:T(8,128)S(1)}, f32[256,128]{1,0:T(8,128)S(1)}, u32[]{:S(2)}, u32[]{:S(2)}) collective-permute-start(f32[256,128]{1,0:T(8,128)S(1)} %bitcast.113), channel_id=1, source_target_pairs={{1,0},{2,1},{3,2},{4,3},{5,4},{6,5},{7,6},{8,7},{9,8},{10,9},{11,1... | collective-permute-start | bytes 393224 | tf_op jit(solution)/shard_map/ppermute | solution.py:17
  20.7 0.8 collective-permute-done.1
  21.7 1.1 convert_bitcast_fusion
  23.0 0.6 fusion.49
  23.6 0.6 copy-done.1
  24.3 3.4 %fusion.30 = f32[6,128,128]{2,0,1:T(8,128)S(1)} fusion(f32[27,2,128,128]{3,2,1,0:T(8,128)S(1)} %bitcast.99, s32[27,2]{0,1:T(2,128)S(1)} %copy-done.14), kind=kOutput, calls=%fused_computation.30 | convolution fusion | flops 63701316 | bytes 3932376 | tf_op jit(solution)/shard_map/kis,kirc->src/dot_general | solution.py:72
  27.8 1.9 %collective-permute-start.2 = (f32[256,128]{1,0:T(8,128)S(1)}, f32[256,128]{1,0:T(8,128)S(1)}, u32[]{:S(2)}, u32[]{:S(2)}) collective-permute-start(f32[256,128]{1,0:T(8,128)S(1)} %bitcast.114), channel_id=1, source_target_pairs={{0,1},{1,2},{2,3},{3,4},{4,5},{5,6},{6,7},{7,8},{8,9},{9,10},{10,1... | collective-permute-start | bytes 393224 | tf_op jit(solution)/shard_map/ppermute | solution.py:15
  29.8 2.4 %collective-permute-start.3 = (f32[256,128]{1,0:T(8,128)S(1)}, f32[256,128]{1,0:T(8,128)S(1)}, u32[]{:S(2)}, u32[]{:S(2)}) collective-permute-start(f32[256,128]{1,0:T(8,128)S(1)} %bitcast.115), channel_id=1, source_target_pairs={{1,0},{2,1},{3,2},{4,3},{5,4},{6,5},{7,6},{8,7},{9,8},{10,9},{11,1... | collective-permute-start | bytes 393224 | tf_op jit(solution)/shard_map/ppermute | solution.py:17
  32.7 3.6 %collective-permute-done.3 = f32[256,128]{1,0:T(8,128)S(1)} collective-permute-done((f32[256,128]{1,0:T(8,128)S(1)}, f32[256,128]{1,0:T(8,128)S(1)}, u32[]{:S(2)}, u32[]{:S(2)}) %collective-permute-start.3) | collective-permute-done | bytes 131104 | tf_op jit(solution)/shard_map/ppermute | solution.py:17
  36.5 1.9 %collective-permute-start.4 = (bf16[256,128]{1,0:T(8,128)(2,1)S(1)}, bf16[256,128]{1,0:T(8,128)(2,1)S(1)}, u32[]{:S(2)}, u32[]{:S(2)}) collective-permute-start(bf16[256,128]{1,0:T(8,128)(2,1)S(1)} %get-tuple-element.7), channel_id=1, source_target_pairs={{0,1},{1,2},{2,3},{3,4},{4,5},{5,6},{6,7},{7,8},{8,9},{9,10},{10,1... | collective-permute-start | bytes 196616 | tf_op jit(solution)/shard_map/ppermute | solution.py:15
  38.4 2.6 %collective-permute-start.5 = (bf16[256,128]{1,0:T(8,128)(2,1)S(1)}, bf16[256,128]{1,0:T(8,128)(2,1)S(1)}, u32[]{:S(2)}, u32[]{:S(2)}) collective-permute-start(bf16[256,128]{1,0:T(8,128)(2,1)S(1)} %get-tuple-element.7), channel_id=1, source_target_pairs={{1,0},{2,1},{3,2},{4,3},{5,4},{6,5},{7,6},{8,7},{9,8},{10,9},{11,1... | collective-permute-start | bytes 196616 | tf_op jit(solution)/shard_map/ppermute | solution.py:17
  41.0 3.3 %collective-permute-done.5 = bf16[256,128]{1,0:T(8,128)(2,1)S(1)} collective-permute-done((bf16[256,128]{1,0:T(8,128)(2,1)S(1)}, bf16[256,128]{1,0:T(8,128)(2,1)S(1)}, u32[]{:S(2)}, u32[]{:S(2)}) %collective-permute-start.5) | collective-permute-done | bytes 65568 | tf_op jit(solution)/shard_map/ppermute | solution.py:17
  44.3 2.0 %gather_fusion = bf16[54,128,128]{2,1,0:T(8,128)(2,1)} fusion(bf16[6,128,128]{2,1,0:T(8,128)(2,1)S(1)} %bitcast.97, s32[1024]{0:T(1024)S(1)} %pad_clamp_fusion), kind=kCustom, calls=%fused_computation.clone | custom fusion | bytes 3539160 | tf_op jit(solution)/shard_map/jit(_take)/gather | solution.py:97
  46.3 1.7 broadcast_select_fusion
  48.0 0.6 fusion.50
  48.7 2.5 %fusion.6 = f32[2,128,128,1]{2,1,3,0:T(8,128)S(1)} fusion(f32[27,2,128,128]{3,2,1,0:T(8,128)S(1)} %bitcast.109, s32[27,2,128]{2,0,1:T(8,128)S(1)} %copy.62, pred[27,2,128]{2,0,1:T(8,128)(4,1)S(1)} %copy.63), kind=kOutput, calls=%fused_computation.8 | convolution fusion | flops 1360723968 | bytes 3704576 | tf_op jit(solution)/shard_map/kbrs,kbrc->bsc/dot_general | solution.py:101
  51.2 0.7 fusion.35
  52.0 1.9 %collective-permute-start.6 = (bf16[256,128]{1,0:T(8,128)(2,1)S(1)}, bf16[256,128]{1,0:T(8,128)(2,1)S(1)}, u32[]{:S(2)}, u32[]{:S(2)}) collective-permute-start(bf16[256,128]{1,0:T(8,128)(2,1)S(1)} %get-tuple-element.15), channel_id=1, source_target_pairs={{0,1},{1,2},{2,3},{3,4},{4,5},{5,6},{6,7},{7,8},{8,9},{9,10},{10,1... | collective-permute-start | bytes 196616 | tf_op jit(solution)/shard_map/ppermute | solution.py:15
  53.9 2.4 %collective-permute-start.7 = (bf16[256,128]{1,0:T(8,128)(2,1)S(1)}, bf16[256,128]{1,0:T(8,128)(2,1)S(1)}, u32[]{:S(2)}, u32[]{:S(2)}) collective-permute-start(bf16[256,128]{1,0:T(8,128)(2,1)S(1)} %get-tuple-element.15), channel_id=1, source_target_pairs={{1,0},{2,1},{3,2},{4,3},{5,4},{6,5},{7,6},{8,7},{9,8},{10,9},{11,1... | collective-permute-start | bytes 196616 | tf_op jit(solution)/shard_map/ppermute | solution.py:17
  56.3 1.6 convolution_convert_fusion
  57.9 4.3 %collective-permute-done.7 = bf16[256,128]{1,0:T(8,128)(2,1)S(1)} collective-permute-done((bf16[256,128]{1,0:T(8,128)(2,1)S(1)}, bf16[256,128]{1,0:T(8,128)(2,1)S(1)}, u32[]{:S(2)}, u32[]{:S(2)}) %collective-permute-start.7) | collective-permute-done | bytes 65568 | tf_op jit(solution)/shard_map/ppermute | solution.py:17
  62.2 2.1 %gather_fusion.1 = bf16[54,128,128]{2,1,0:T(8,128)(2,1)} fusion(bf16[6,128,128]{2,1,0:T(8,128)(2,1)S(1)} %bitcast.96, s32[1024]{0:T(1024)S(1)} %pad_clamp_fusion), kind=kCustom, calls=%fused_computation.1.clone | custom fusion | bytes 3539160 | tf_op jit(solution)/shard_map/jit(_take)/gather | solution.py:97
  64.2 1.7 broadcast_select_fusion.1
  66.0 0.7 convolution_convert_fusion.1
  67.9 27.9 %all_to_all.17 = bf16[16,2,216,128]{3,2,1,0:T(8,128)(2,1)} all-to-all(bf16[16,2,216,128]{3,2,1,0:T(8,128)(2,1)S(1)} %maximum_bitcast_fusion), channel_id=1, replica_groups=mesh['grp'=16,'tile'=32] {'grp'}, dimensions={0} | all-to-all | bytes 3538944 | tf_op jit(solution)/shard_map/all_to_all | solution.py:31
  95.9 2.5 %reduce_sum.21 = bf16[2,216,128]{2,1,0:T(8,128)(2,1)} reduce(bf16[16,2,216,128]{3,2,1,0:T(8,128)(2,1)} %all_to_all.17, bf16[]{:T(256)} %constant.10.clone.1), dimensions={0}, to_apply=%region_0.2 | reduce | flops 829440 | bytes 1880066 | tf_op jit(solution)/shard_map/reduce_sum | solution.py:32
  98.4 1.8 %convert_element_type.86 = bf16[32,1,1728]{2,1,0:T(2,128)(2,1)} reshape(bf16[2,216,128]{2,1,0:T(8,128)(2,1)} %reduce_sum.21) | data formatting | bytes 221184 | tf_op jit(solution)/shard_map/convert_element_type | solution.py:142
  100.7 2.9 %reduce.6 = bf16[32,1728]{1,0:T(8,128)(2,1)} reduce(bf16[32,1,1728]{2,1,0:T(2,128)(2,1)} %convert_element_type.86, bf16[]{:T(256)} %broadcast.28), dimensions={1}, to_apply=%convert_element_type.86.reduce_sub_computation | reduce | bytes 221186 | tf_op jit(solution)/shard_map/convert_element_type | solution.py:142
  103.6 1.7 reshape.175
  105.3 32.9 %all_to_all.18 = bf16[32,2,864]{2,1,0:T(2,128)(2,1)} all-to-all(bf16[32,2,864]{2,1,0:T(2,128)(2,1)} %reshape.175), channel_id=1, replica_groups=mesh['grp'=16,'tile'=32] {'tile'}, dimensions={0} | all-to-all | bytes 221184 | tf_op jit(solution)/shard_map/all_to_all | solution.py:31
  138.2 1.8 %reshape.176 = bf16[32,1,1728]{2,1,0:T(2,128)(2,1)} reshape(bf16[32,2,864]{2,1,0:T(2,128)(2,1)} %all_to_all.18) | data formatting | bytes 221184
  140.0 1.2 convert_reduce_fusion
  141.2 0.8 broadcast_in_dim.11
  142.0 5.8 %all-to-all-start.2 = ((f32[32,1,1728]{2,1,0:T(1,128)}), f32[32,1,1728]{2,1,0:T(1,128)}, u32[]{:S(2)}, u32[]{:S(2)}) async-start(f32[32,1,1728]{2,1,0:T(1,128)} %broadcast_in_dim.11), calls=%async_computation.2 | async-start | bytes 458752 | tf_op jit(solution)/shard_map/all_to_all | solution.py:43
  147.8 0.6 fusion.51
  148.5 2.5 %fusion.4 = f32[2,128,128,1]{2,1,3,0:T(8,128)S(1)} fusion(f32[27,2,128,128]{3,2,1,0:T(8,128)S(1)} %bitcast.108, s32[27,2,128]{2,0,1:T(8,128)S(1)} %copy-done.11, pred[27,2,128]{2,0,1:T(8,128)(4,1)S(1)} %copy.63), kind=kOutput, calls=%fused_computation.6 | convolution fusion | flops 1360723968 | bytes 3704576 | tf_op jit(solution)/shard_map/kbrs,kbrc->bsc/dot_general | solution.py:101
  151.1 0.6 fusion.33
  151.7 16.5 %all-to-all-done.2 = f32[32,1,1728]{2,1,0:T(1,128)} async-done(((f32[32,1,1728]{2,1,0:T(1,128)}), f32[32,1,1728]{2,1,0:T(1,128)}, u32[]{:S(2)}, u32[]{:S(2)}) %all-to-all-start.2) | async-done | bytes 221216 | tf_op jit(solution)/shard_map/all_to_all | solution.py:43
  168.2 1.2 broadcast_multiply_fusion
  169.4 0.6 slice_reduce_fusion
  170.0 0.7 squeeze.34
  170.8 0.7 squeeze.35
  (64 shorter events, 4.3 us)
Async XLA Ops:
  0.6 22.4 %copy-start = (bf16[27,128,128]{2,1,0:T(8,128)(2,1)S(1)}, bf16[27,128,128]{2,1,0:T(8,128)(2,1)}, u32[]{:S(2)}) copy-start(bf16[27,128,128]{2,1,0:T(8,128)(2,1)} %param.14) | copy-start | bytes 2654212
  2.1 46.5 %copy-start.10 = (s32[27,2,128]{2,0,1:T(8,128)}, s32[27,2,128]{2,0,1:T(8,128)S(1)}, u32[]{:S(2)}) copy-start(s32[27,2,128]{2,0,1:T(8,128)S(1)} %copy.62) | copy-start | bytes 82948
  4.9 1.2 copy-start.5
  6.1 0.7 copy-start.14
  10.3 10.4 %collective-permute-start = (f32[256,128]{1,0:T(8,128)S(1)}, f32[256,128]{1,0:T(8,128)S(1)}, u32[]{:S(2)}, u32[]{:S(2)}) collective-permute-start(f32[256,128]{1,0:T(8,128)S(1)} %bitcast.112), channel_id=1, source_target_pairs={{0,1},{1,2},{2,3},{3,4},{4,5},{5,6},{6,7},{7,8},{8,9},{9,10},{10,1... | collective-permute-start | bytes 393224 | tf_op jit(solution)/shard_map/ppermute | solution.py:15
  15.3 6.3 %collective-permute-start.1 = (f32[256,128]{1,0:T(8,128)S(1)}, f32[256,128]{1,0:T(8,128)S(1)}, u32[]{:S(2)}, u32[]{:S(2)}) collective-permute-start(f32[256,128]{1,0:T(8,128)S(1)} %bitcast.113), channel_id=1, source_target_pairs={{1,0},{2,1},{3,2},{4,3},{5,4},{6,5},{7,6},{8,7},{9,8},{10,9},{11,1... | collective-permute-start | bytes 393224 | tf_op jit(solution)/shard_map/ppermute | solution.py:17
  20.7 2.3 %copy-start.16 = (s32[54]{0:T(128)}, s32[54]{0:T(128)S(1)}, u32[]{:S(2)}) copy-start(s32[54]{0:T(128)S(1)} %reshape.136) | copy-start | bytes 652
  23.0 1.3 copy-start.1
  24.3 7.9 %copy-start.17 = (s32[54]{0:T(128)S(1)}, s32[54]{0:T(128)}, u32[]{:S(2)}) copy-start(s32[54]{0:T(128)} %copy-done.16) | copy-start | bytes 652
  24.3 12.1 %copy-start.12 = (bf16[256,128]{1,0:T(8,128)(2,1)S(1)}, bf16[256,128]{1,0:T(8,128)(2,1)}, u32[]{:S(2)}) copy-start(bf16[256,128]{1,0:T(8,128)(2,1)} %param.15) | copy-start | bytes 196612
  24.3 12.1 %copy-start.13 = (bf16[256,128]{1,0:T(8,128)(2,1)S(1)}, bf16[256,128]{1,0:T(8,128)(2,1)}, u32[]{:S(2)}) copy-start(bf16[256,128]{1,0:T(8,128)(2,1)} %param.9) | copy-start | bytes 196612
  27.8 4.9 %collective-permute-start.2 = (f32[256,128]{1,0:T(8,128)S(1)}, f32[256,128]{1,0:T(8,128)S(1)}, u32[]{:S(2)}, u32[]{:S(2)}) collective-permute-start(f32[256,128]{1,0:T(8,128)S(1)} %bitcast.114), channel_id=1, source_target_pairs={{0,1},{1,2},{2,3},{3,4},{4,5},{5,6},{6,7},{7,8},{8,9},{9,10},{10,1... | collective-permute-start | bytes 393224 | tf_op jit(solution)/shard_map/ppermute | solution.py:15
  29.8 6.6 %collective-permute-start.3 = (f32[256,128]{1,0:T(8,128)S(1)}, f32[256,128]{1,0:T(8,128)S(1)}, u32[]{:S(2)}, u32[]{:S(2)}) collective-permute-start(f32[256,128]{1,0:T(8,128)S(1)} %bitcast.115), channel_id=1, source_target_pairs={{1,0},{2,1},{3,2},{4,3},{5,4},{6,5},{7,6},{8,7},{9,8},{10,9},{11,1... | collective-permute-start | bytes 393224 | tf_op jit(solution)/shard_map/ppermute | solution.py:17
  36.4 7.8 %copy-start.8 = (bf16[256,128]{1,0:T(8,128)(2,1)}, bf16[256,128]{1,0:T(8,128)(2,1)S(1)}, u32[]{:S(2)}) copy-start(bf16[256,128]{1,0:T(8,128)(2,1)S(1)} %get-tuple-element.7) | copy-start | bytes 196612
  36.5 4.5 %collective-permute-start.4 = (bf16[256,128]{1,0:T(8,128)(2,1)S(1)}, bf16[256,128]{1,0:T(8,128)(2,1)S(1)}, u32[]{:S(2)}, u32[]{:S(2)}) collective-permute-start(bf16[256,128]{1,0:T(8,128)(2,1)S(1)} %get-tuple-element.7), channel_id=1, source_target_pairs={{0,1},{1,2},{2,3},{3,4},{4,5},{5,6},{6,7},{7,8},{8,9},{9,10},{10,1... | collective-permute-start | bytes 196616 | tf_op jit(solution)/shard_map/ppermute | solution.py:15
  38.4 5.9 %collective-permute-start.5 = (bf16[256,128]{1,0:T(8,128)(2,1)S(1)}, bf16[256,128]{1,0:T(8,128)(2,1)S(1)}, u32[]{:S(2)}, u32[]{:S(2)}) collective-permute-start(bf16[256,128]{1,0:T(8,128)(2,1)S(1)} %get-tuple-element.7), channel_id=1, source_target_pairs={{1,0},{2,1},{3,2},{4,3},{5,4},{6,5},{7,6},{8,7},{9,8},{10,9},{11,1... | collective-permute-start | bytes 196616 | tf_op jit(solution)/shard_map/ppermute | solution.py:17
  44.3 2.0 %copy-start.15 = (pred[54]{0:T(512)(128)(4,1)S(1)}, pred[54]{0:T(512)(128)(4,1)}, u32[]{:S(2)}) copy-start(pred[54]{0:T(512)(128)(4,1)} %compare_and_fusion.1) | copy-start | bytes 166
  48.7 7.6 %copy-start.2 = (bf16[27,2,128,128]{3,2,1,0:T(8,128)(2,1)S(1)}, bf16[27,2,128,128]{3,2,1,0:T(8,128)(2,1)}, u32[]{:S(2)}) copy-start(bf16[27,2,128,128]{3,2,1,0:T(8,128)(2,1)} %copy-done.1) | copy-start | bytes 5308420
  52.0 6.0 %collective-permute-start.6 = (bf16[256,128]{1,0:T(8,128)(2,1)S(1)}, bf16[256,128]{1,0:T(8,128)(2,1)S(1)}, u32[]{:S(2)}, u32[]{:S(2)}) collective-permute-start(bf16[256,128]{1,0:T(8,128)(2,1)S(1)} %get-tuple-element.15), channel_id=1, source_target_pairs={{0,1},{1,2},{2,3},{3,4},{4,5},{5,6},{6,7},{7,8},{8,9},{9,10},{10,1... | collective-permute-start | bytes 196616 | tf_op jit(solution)/shard_map/ppermute | solution.py:15
  53.9 8.3 %collective-permute-start.7 = (bf16[256,128]{1,0:T(8,128)(2,1)S(1)}, bf16[256,128]{1,0:T(8,128)(2,1)S(1)}, u32[]{:S(2)}, u32[]{:S(2)}) collective-permute-start(bf16[256,128]{1,0:T(8,128)(2,1)S(1)} %get-tuple-element.15), channel_id=1, source_target_pairs={{1,0},{2,1},{3,2},{4,3},{5,4},{6,5},{7,6},{8,7},{9,8},{10,9},{11,1... | collective-permute-start | bytes 196616 | tf_op jit(solution)/shard_map/ppermute | solution.py:17
  66.0 1.3 copy-start.3
  66.0 1.8 %copy-start.7 = (bf16[27,128,128]{2,1,0:T(8,128)(2,1)S(1)}, bf16[27,128,128]{2,1,0:T(8,128)(2,1)}, u32[]{:S(2)}) copy-start(bf16[27,128,128]{2,1,0:T(8,128)(2,1)} %convolution_convert_fusion) | copy-start | bytes 2654212
  95.9 51.9 %copy-start.4 = (bf16[54,128,128]{2,1,0:T(8,128)(2,1)S(1)}, bf16[54,128,128]{2,1,0:T(8,128)(2,1)}, u32[]{:S(2)}) copy-start(bf16[54,128,128]{2,1,0:T(8,128)(2,1)} %copy-done.3) | copy-start | bytes 5308420
  95.9 51.9 %copy-start.6 = (bf16[27,128,128]{2,1,0:T(8,128)(2,1)S(1)}, bf16[27,128,128]{2,1,0:T(8,128)(2,1)}, u32[]{:S(2)}) copy-start(bf16[27,128,128]{2,1,0:T(8,128)(2,1)} %param.13) | copy-start | bytes 2654212
  142.0 26.2 %all-to-all-start.2 = ((f32[32,1,1728]{2,1,0:T(1,128)}), f32[32,1,1728]{2,1,0:T(1,128)}, u32[]{:S(2)}, u32[]{:S(2)}) async-start(f32[32,1,1728]{2,1,0:T(1,128)} %broadcast_in_dim.11), calls=%async_computation.2 | async-start | bytes 458752 | tf_op jit(solution)/shard_map/all_to_all | solution.py:43
  147.8 0.8 copy-start.11
  148.5 2.5 %copy-start.9 = (bf16[256,128]{1,0:T(8,128)(2,1)S(1)}, bf16[256,128]{1,0:T(8,128)(2,1)}, u32[]{:S(2)}) copy-start(bf16[256,128]{1,0:T(8,128)(2,1)} %copy-done.8) | copy-start | bytes 196612
where the time goes:
time: 173 us; the launch traced here: 172 us
  blocking collectives  60.9 us (35%)
  starting transfers between devices  28.9 us (17%)
  waiting for transfers between devices  28.4 us (16%)
  matrix products  19.7 us (11%)
  local copies, waits for them, and re-layouts  17.5 us (10%)
  other arithmetic  14.3 us (8%)
  between operations  1.8 us (1%)
    all_to_all x2, blocking collectives, sent_and_summed(): lax.all_to_all(pieces, axis, split_axis=0, concat_axis=0, tiled=True)  60.9 us
    all_to_all x1, waiting for transfers between devices, from_everyone(): lax.all_to_all(jnp.broadcast_to(value[None], (count, *value.shape)), axis...  16.5 us
    ppermute x4, starting transfers between devices, padded_2(): lax.ppermute(head, axis, [((i + 1) % count, i) for i in range(ends)])  12.5 us
    ppermute x4, waiting for transfers between devices, padded_2(): lax.ppermute(head, axis, [((i + 1) % count, i) for i in range(ends)])  11.9 us
    ppermute x4, starting transfers between devices, padded_2(): lax.ppermute(tail, axis, [(i, (i + 1) % count) for i in range(ends)])  10.7 us
    unnamed x40, local copies, waits for them, and re-layouts  7.37 us
    dot_general x2, matrix products, spread_terms(): jnp.einsum('kis,kirc->src', one_hot, partial_value.reshape(offsets, block...  6.78 us
    all_to_all x1, starting transfers between devices, from_everyone(): lax.all_to_all(jnp.broadcast_to(value[None], (count, *value.shape)), axis...  5.75 us
  transfers between devices with their start and end apart: 9, of which 5 were waited for; matrix products, arithmetic and copies ran while one was open for 4% of the time, Pallas kernels for 0%

commit v1 on v0

v1 whole, which is shorter than its diff:
```python
import functools
import math

import jax
import jax.numpy as jnp
from jax import lax
from jax.experimental import pallas as pl
from jax.experimental.pallas import tpu as pltpu
from jax.sharding import PartitionSpec as P

MESH = pl.DeviceIdType.MESH
BF = jnp.bfloat16
F32 = jnp.float32
I32 = jnp.int32


def nn(a, b):
    return lax.dot_general(a, b, (((1,), (0,)), ((), ())), preferred_element_type=F32)


def nt(a, b):
    return lax.dot_general(a, b, (((1,), (1,)), ((), ())), preferred_element_type=F32)


def silu_parts(v):
    s = 1.0 / (1.0 + jnp.exp(-v))
    return v * s, s * (1.0 + v * (1.0 - s))


def kernel(
    dims,
    feat,
    src,
    codes,
    count,
    w_one,
    w_two,
    cot,
    out_ref,
    dx_ref,
    wg_one,
    wg_two,
    ot,
    pt,
    gt,
    wraw,
    wt,
    wc,
    ht,
    hid,
    pre,
    q,
    xs,
    xr,
    qe,
    wgf,
    cs,
    cr,
    sx,
    rx,
    ab,
    bb,
    fb,
    w_sem,
    x_send,
    x_recv,
    c_send,
    c_recv,
    g_send,
    g_recv,
    a_send,
    a_recv,
    b_send,
    b_recv,
    f_send,
    f_recv,
):
    n_grp, n_tile, kvol, rows_k, side, zside = dims
    third = kvol // 3
    B = rows_k
    shard = kvol * B // n_grp
    half = cs.shape[2]
    g = lax.axis_index("grp")
    t = lax.axis_index("tile")
    nz = n_tile // 2
    z = t // 2
    core = t % 2
    gy = g // side
    gx = g % side
    left = lax.rem(t + n_tile - 1, n_tile)
    right = lax.rem(t + 1, n_tile)
    sib = t + 1 - 2 * core
    zlo = z % zside
    zhi = z // zside

    def grp_of(o):
        dy, dx = o // side, o % side
        return lax.rem(gy + dy, side) * side + lax.rem(gx + dx, side)

    def near_z(d):
        return (zhi * zside + lax.rem(zlo + d, zside)) * 2 + core

    def far_z(d):
        return (lax.rem(zhi + d, zside) * zside + zlo) * 2 + core

    for k, w in ((0, w_one), (1, w_two)):
        pltpu.make_async_copy(w, wraw.at[k], w_sem.at[k]).start()

    barrier = pltpu.get_barrier_semaphore()
    partners = [{"tile": left}, {"tile": right}]
    partners += [{"grp": grp_of(o)} for o in range(1, n_grp)]
    partners += [{"tile": near_z(d)} for d in range(1, zside)]
    partners += [{"tile": far_z(d)} for d in range(1, zside)]
    for p in partners:
        pl.semaphore_signal(barrier, inc=1, device_id=p, device_id_type=MESH)

    two = count[0] - 1
    two_f = two.astype(F32)
    one_f = 1.0 - two_f
    keep_prev = jnp.where(t == 0, 0.0, 1.0)
    keep_next = jnp.where(t == n_tile - 1, 0.0, 1.0)

    for j in range(2):
        ht[:, j * B : (j + 1) * B] = feat[j * B : (j + 1) * B, :].T

    iota = lax.broadcasted_iota(I32, (B, B), 0)

    def onehot(k, carry):
        for j in range(2):
            row = src[k, pl.ds(j, 1), :]
            high = codes[k, j] & 1
            live = two if j else 1
            for b in range(2):
                m = (high if b else 1 - high) * live
                idx = row * m + (m - 1)
                hit = jnp.where(iota == idx, 1.0, 0.0).astype(BF)
                ot[k, j * B : (j + 1) * B, b * B : (b + 1) * B] = hit
        return carry

    lax.fori_loop(0, kvol, onehot, 0)

    def prep(w):
        pltpu.make_async_copy(w_two if w else w_one, wraw.at[w], w_sem.at[w]).wait()

        def body(i, carry):
            for pos, cls in enumerate((1, 0, 2)):
                at = pl.multiple_of((pos * third + i) * B, B)
                block = wraw[w, 3 * i + cls]
                wc[w, :, pl.ds(at, B)] = block
                wt[w, :, pl.ds(at, B)] = block.T
            return carry

        lax.fori_loop(0, third, body, 0)

    n1 = third * B

    def put(slot, i, value):
        at = pl.multiple_of((slot * third + i) * B, B)
        pt[pl.ds(at, B), :] = value.astype(BF)

    def forward_edges(field, w):
        def body(i, carry):
            put(2, i, nn(field[:, :B], ot[3 * i, :B, :]))
            put(3, i, nn(field[:, :B], ot[3 * i + 2, :B, :]))
            put(4, i, nn(field[:, B:], ot[3 * i + 2, B:, :]))
            return carry

        lax.fori_loop(0, third, body, 0)
        to_prev = nn(wt[w, :, n1 : 2 * n1], pt[2 * n1 : 3 * n1, :])
        part_a = nn(wt[w, :, 2 * n1 :], pt[3 * n1 : 4 * n1, :])
        part_b = nn(wt[w, :, 2 * n1 :], pt[4 * n1 :, :])
        xs[w, 0] = to_prev.astype(BF)
        xs[w, 1] = (part_b + part_a * one_f).astype(BF)
        return part_a * two_f

    def forward_own(field, w):
        def body(i, carry):
            put(0, i, nn(field[...], ot[3 * i + 1]))
            put(1, i, nn(field[:, B:], ot[3 * i, B:, :]))
            return carry

        lax.fori_loop(0, third, body, 0)
        return nn(wt[w, :, : 2 * n1], pt[: 2 * n1, :])

    def exchange(e, to_prev, to_next):
        return [
            pltpu.make_async_remote_copy(
                src_ref=to_prev,
                dst_ref=xr.at[e, 1],
                send_sem=x_send.at[e, 1],
                recv_sem=x_recv.at[e, 1],
                device_id={"tile": left},
                device_id_type=MESH,
            ),
            pltpu.make_async_remote_copy(
                src_ref=to_next,
                dst_ref=xr.at[e, 0],
                send_sem=x_send.at[e, 0],
                recv_sem=x_recv.at[e, 0],
                device_id={"tile": right},
                device_id_type=MESH,
            ),
        ]

    def from_sides(e):
        return (
            xr[e, 0].astype(F32) * keep_prev,
            xr[e, 1].astype(F32) * keep_next,
        )

    def start(copies):
        for c in copies:
            c.start()
        return copies

    def landed(copies):
        for c in copies:
            c.wait_recv()

    pending = []
    mask = jnp.where(
        lax.broadcasted_iota(I32, (1, 2 * B), 1) < B * count[0], 1.0, 0.0
    )

    prep(0)
    extra = forward_edges(ht, 0)
    pl.semaphore_wait(barrier, len(partners))
    moved = start(exchange(0, xs.at[0, 0], xs.at[0, 1]))
    pending += moved
    own = forward_own(ht, 0) + extra
    prep(1)
    landed(moved)
    before, after = from_sides(0)
    pre_one = own + before + after
    pre[...] = pre_one
    hid[...] = (silu_parts(pre_one)[0] * mask).astype(BF)

    extra = forward_edges(hid, 1)
    moved = start(exchange(1, xs.at[1, 0], xs.at[1, 1]))
    pending += moved
    own = forward_own(hid, 1) + extra + ht[...].astype(F32)
    cot_t = jnp.concatenate(
        [cot[:B, :].astype(F32).T, cot[B:, :].astype(F32).T], axis=1
    )
    landed(moved)
    before, after = from_sides(1)
    total = own + before + after
    value, slope = silu_parts(total)
    q[1] = (cot_t * slope * mask).astype(BF)
    moved = start(exchange(2, q.at[1], q.at[1]))
    pending += moved
    result = value * mask
    for j in range(2):
        out_ref[j * B : (j + 1) * B, :] = result[:, j * B : (j + 1) * B].T.astype(BF)

    def put_g(pos, i, lo, hi, v):
        at = pl.multiple_of((pos * third + i) * B, B)
        gt[pl.ds(at, B), lo:hi] = v.astype(BF)

    def back_own(w):
        def body(i, carry):
            put_g(0, i, 0, 2 * B, nt(q[w], ot[3 * i + 1]))
            put_g(1, i, B, 2 * B, nt(q[w], ot[3 * i, B:, :]))
            return carry

        lax.fori_loop(0, third, body, 0)

    def back_edges(w, e):
        before, after = from_sides(e)
        mixed = (after * one_f + q[w].astype(F32) * two_f).astype(BF)
        before = before.astype(BF)
        after = after.astype(BF)
        qe[0] = before
        qe[1] = mixed
        qe[2] = after

        def body(i, carry):
            put_g(1, i, 0, B, nt(qe[0], ot[3 * i, :B, :]))
            put_g(2, i, 0, B, nt(qe[1], ot[3 * i + 2, :B, :]))
            put_g(2, i, B, 2 * B, nt(qe[2], ot[3 * i + 2, B:, :]))
            return carry

        lax.fori_loop(0, third, body, 0)

    def weight_grads(field, w):
        def body(i, carry):
            for pos, cls in enumerate((1, 0, 2)):
                at = pl.multiple_of((pos * third + i) * B, B)
                to = pl.multiple_of((3 * i + cls) * B, B)
                wgf[w, pl.ds(to, B), :] = nt(field[...], gt[pl.ds(at, B), :])
            return carry

        lax.fori_loop(0, third, body, 0)

    def half_rows(w, s, h):
        at = pl.multiple_of(s * shard + h * half, 8)
        return wgf[w, pl.ds(at, half), :]

    def send_pair(w):
        def body(s, carry):
            cs[w, s] = half_rows(w, s, 1 - core).astype(BF)
            return carry

        lax.fori_loop(0, n_grp, body, 0)
        return start(
            [
                pltpu.make_async_remote_copy(
                    src_ref=cs.at[w],
                    dst_ref=cr.at[w],
                    send_sem=c_send.at[w],
                    recv_sem=c_recv.at[w],
                    device_id={"tile": sib},
                    device_id_type=MESH,
                )
            ]
        )

    def send_plane(w, moved):
        landed(moved)

        def body(s, carry):
            sx[w, s] = (half_rows(w, s, core) + cr[w, s].astype(F32)).astype(BF)
            return carry

        lax.fori_loop(0, n_grp, body, 0)
        return start(
            [
                pltpu.make_async_remote_copy(
                    src_ref=sx.at[w, grp_of(o)],
                    dst_ref=rx.at[w, o],
                    send_sem=g_send.at[w, o],
                    recv_sem=g_recv.at[w, o],
                    device_id={"grp": grp_of(o)},
                    device_id_type=MESH,
                )
                for o in range(1, n_grp)
            ]
        )

    def send_near(w, moved):
        landed(moved)
        acc = sx[w, g].astype(F32)
        for o in range(1, n_grp):
            acc = acc + rx[w, o].astype(F32)
        ab[w, zlo] = acc.astype(BF)
        return start(
            [
                pltpu.make_async_remote_copy(
                    src_ref=ab.at[w, zlo],
                    dst_ref=ab.at[w, zlo],
                    send_sem=a_send.at[w, d],
                    recv_sem=a_recv.at[w, d],
                    device_id={"tile": near_z(d)},
                    device_id_type=MESH,
                )
                for d in range(1, zside)
            ]
        )

    def send_far(w, moved):
        landed(moved)
        acc = ab[w, 0].astype(F32)
        for d in range(1, zside):
            acc = acc + ab[w, d].astype(F32)
        bb[w, zhi] = acc.astype(BF)
        return start(
            [
                pltpu.make_async_remote_copy(
                    src_ref=bb.at[w, zhi],
                    dst_ref=bb.at[w, zhi],
                    send_sem=b_send.at[w, d],
                    recv_sem=b_recv.at[w, d],
                    device_id={"tile": far_z(d)},
                    device_id_type=MESH,
                )
                for d in range(1, zside)
            ]
        )

    def send_last(w, moved):
        landed(moved)
        acc = bb[w, 0].astype(F32)
        for d in range(1, zside):
            acc = acc + bb[w, d].astype(F32)
        fb[w, core] = acc
        return start(
            [
                pltpu.make_async_remote_copy(
                    src_ref=fb.at[w, core],
                    dst_ref=fb.at[w, core],
                    send_sem=f_send.at[w],
                    recv_sem=f_recv.at[w],
                    device_id={"tile": sib},
                    device_id_type=MESH,
                )
            ]
        )

    scale = float(n_grp * n_tile * 2 * B) ** (-0.5)

    def finish(w, moved):
        landed(moved)
        dst = wg_two if w else wg_one
        dst[:half, :] = fb[w, 0] * scale
        dst[half:, :] = fb[w, 1, : shard - half, :] * scale

    for w in range(2 if wgf.shape[1] > kvol * B else 0):
        wgf[w, kvol * B :, :] = jnp.zeros((wgf.shape[1] - kvol * B, B), F32)

    back_own(1)
    landed(moved)
    back_edges(1, 2)
    grad_mid = nn(wc[1], gt[...])
    slope = silu_parts(pre[...])[1]
    q[0] = (grad_mid * slope * mask).astype(BF)
    moved = start(exchange(3, q.at[0], q.at[0]))
    pending += moved
    weight_grads(hid, 1)
    pair_two = send_pair(1)
    back_own(0)
    plane_two = send_plane(1, pair_two)
    landed(moved)
    back_edges(0, 3)
    weight_grads(ht, 0)
    pair_one = send_pair(0)
    grad_in = nn(wc[0], gt[...]) + q[1].astype(F32)
    plane_one = send_plane(0, pair_one)
    for j in range(2):
        dx_ref[j * B : (j + 1) * B, :] = grad_in[:, j * B : (j + 1) * B].T.astype(BF)
    near_two = send_near(1, plane_two)
    near_one = send_near(0, plane_one)
    far_two = send_far(1, near_two)
    far_one = send_far(0, near_one)
    last_two = send_last(1, far_two)
    finish(1, last_two)
    last_one = send_last(0, far_one)
    finish(0, last_one)
    pending += pair_two + plane_two + pair_one + plane_one
    pending += near_two + near_one + far_two + far_one + last_two + last_one
    for c in pending:
        c.wait_send()


def on_device(n_grp, n_tile, features, source_rows, target_codes, block_count, w1, w2, cot):
    kvol, _, B = source_rows.shape
    side = math.isqrt(n_grp)
    zside = math.isqrt(n_tile // 2)
    shard = kvol * B // n_grp
    half = -(-shard // 32) * 16
    wide = kvol * B
    vmem = pl.BlockSpec(memory_space=pltpu.VMEM)
    smem = pl.BlockSpec(memory_space=pltpu.SMEM)
    hbm = pl.BlockSpec(memory_space=pl.ANY)
    dma = pltpu.SemaphoreType.DMA
    dims = (n_grp, n_tile, kvol, B, side, zside)
    return pl.pallas_call(
        functools.partial(kernel, dims),
        out_shape=(
            jax.ShapeDtypeStruct((2 * B, B), BF),
            jax.ShapeDtypeStruct((2 * B, B), BF),
            jax.ShapeDtypeStruct((shard, B), F32),
            jax.ShapeDtypeStruct((shard, B), F32),
        ),
        in_specs=[vmem, vmem, smem, smem, hbm, hbm, vmem],
        out_specs=(vmem,) * 4,
        scratch_shapes=[
            pltpu.VMEM((kvol, 2 * B, 2 * B), BF),
            pltpu.VMEM((5 * (kvol // 3) * B, 2 * B), BF),
            pltpu.VMEM((wide, 2 * B), BF),
            pltpu.VMEM((2, kvol, B, B), BF),
            pltpu.VMEM((2, B, wide), BF),
            pltpu.VMEM((2, B, wide), BF),
            pltpu.VMEM((B, 2 * B), BF),
            pltpu.VMEM((B, 2 * B), BF),
            pltpu.VMEM((B, 2 * B), F32),
            pltpu.VMEM((2, B, 2 * B), BF),
            pltpu.VMEM((2, 2, B, 2 * B), BF),
            pltpu.VMEM((4, 2, B, 2 * B), BF),
            pltpu.VMEM((3, B, 2 * B), BF),
            pltpu.VMEM((2, wide + 2 * half - shard, B), F32),
            pltpu.VMEM((2, n_grp, half, B), BF),
            pltpu.VMEM((2, n_grp, half, B), BF),
            pltpu.VMEM((2, n_grp, half, B), BF),
            pltpu.VMEM((2, n_grp, half, B), BF),
            pltpu.VMEM((2, zside, half, B), BF),
            pltpu.VMEM((2, zside, half, B), BF),
            pltpu.VMEM((2, 2, half, B), F32),
            dma((2,)),
            dma((4, 2)),
            dma((4, 2)),
            dma((2,)),
            dma((2,)),
            dma((2, n_grp)),
            dma((2, n_grp)),
            dma((2, zside)),
            dma((2, zside)),
            dma((2, zside)),
            dma((2, zside)),
            dma((2,)),
            dma((2,)),
        ],
        compiler_params=pltpu.CompilerParams(
            collective_id=0, has_side_effects=True, vmem_limit_bytes=48 * 1024 * 1024
        ),
    )(features, source_rows, target_codes, block_count, w1, w2, cot)


def solution(mesh):
    n_grp, n_tile = mesh.shape["grp"], mesh.shape["tile"]
    rows = P(("grp", "tile"), None)
    return jax.shard_map(
        functools.partial(on_device, n_grp, n_tile),
        mesh=mesh,
        in_specs=(
            rows,
            P(None, ("grp", "tile"), None),
            P(None, ("grp", "tile")),
            P(("grp", "tile")),
            P(),
            P(),
            rows,
        ),
        out_specs=(rows, rows, P("grp", None), P("grp", None)),
        check_vma=False,
    )
```

time: 173 us -> 76.7 us (0.44)
  Pallas kernels: 0 us -> 67.6 us
  blocking collectives: 60.9 us -> 0 us
  starting transfers between devices: 28.9 us -> 0 us
  waiting for transfers between devices: 28.4 us -> 0 us
  matrix products: 19.7 us -> 0 us
  other arithmetic: 14.3 us -> 0 us
  local copies, waits for them, and re-layouts: 17.5 us -> 7.42 us
    pallas_call x0 -> x1, Pallas kernels: none -> 67.6 us  [on_device(): pl.pallas_call(functools.partial(kernel, dims), out_shape=(jax.ShapeDtype...]
    all_to_all x2 -> x0, blocking collectives: 60.9 us -> none  [sent_and_summed(): lax.all_to_all(pieces, axis, split_axis=0, concat_axis=0, tiled=True)]
    ppermute x8 -> x0, starting transfers between devices: 23.2 us -> none  [the longest x4 12.5 us: padded_2(): lax.ppermute(head, axis, [((i + 1) % count, i) for i in range(ends)])]
    dot_general x12 -> x0, matrix products: 19.7 us -> none  [the longest x2 6.78 us: spread_terms(): jnp.einsum('kis,kirc->src', one_hot, partial_value.reshape(offsets, block...]
    all_to_all x1 -> x0, waiting for transfers between devices: 16.5 us -> none  [from_everyone(): lax.all_to_all(jnp.broadcast_to(value[None], (count, *value.shape)), axis...]
    ppermute x8 -> x0, waiting for transfers between devices: 12 us -> none  [the longest x4 11.9 us: padded_2(): lax.ppermute(head, axis, [((i + 1) % count, i) for i in range(ends)])]
    all_to_all x1 -> x0, starting transfers between devices: 5.75 us -> none  [from_everyone(): lax.all_to_all(jnp.broadcast_to(value[None], (count, *value.shape)), axis...]
    convert_element_type x6 -> x0, other arithmetic: 4.47 us -> none  [the longest x1 2.88 us: on_device(): summed_piece = sent_and_summed(flat_part.astype(jnp.bfloat16), 'tile', 0)]
  transfers between devices with their start and end apart: 9 -> 0, of which waited for: 5 -> 0; matrix products, arithmetic and copies ran while one was open for 4% -> 0% of each run, Pallas kernels for 0% -> 0%
where the time goes in v1:
time: 76.7 us; the launch traced here: 76.3 us
  Pallas kernels  67.6 us (88%)
  local copies, waits for them, and re-layouts  7.42 us (10%)
  between operations  1.31 us (2%)
    pallas_call x1, Pallas kernels, on_device(): pl.pallas_call(functools.partial(kernel, dims), out_shape=(jax.ShapeDtype...  67.6 us
    unnamed x17, local copies, waits for them, and re-layouts  7.42 us

profile of v1, /device:TPU:1, one launch (start us, length us, event | category | flops | bytes accessed | tf_op | source)
XLA Modules:
  0.0 76.3 jit_solution(2068650936434505457)
XLA Ops:
  0.6 0.0 copy-start.5
  1.3 0.0 copy-done.5
  1.3 0.1 copy.11.codes
  1.4 0.0 copy-start
  1.4 1.2 %copy-done = bf16[27,128,128]{2,1,0:T(8,128)(2,1)S(1)} copy-done((bf16[27,128,128]{2,1,0:T(8,128)(2,1)S(1)}, bf16[27,128,128]{2,1,0:T(8,128)(2,1)}, u32[]{:S(2)}) %copy-start) | copy-done | bytes 884760
  2.6 0.0 copy-start.1
  2.6 1.2 %copy-done.1 = bf16[27,128,128]{2,1,0:T(8,128)(2,1)S(1)} copy-done((bf16[27,128,128]{2,1,0:T(8,128)(2,1)S(1)}, bf16[27,128,128]{2,1,0:T(8,128)(2,1)}, u32[]{:S(2)}) %copy-start.1) | copy-done | bytes 884760
  3.7 0.0 copy-start.2
  3.7 0.8 %copy-done.2 = bf16[256,128]{1,0:T(8,128)(2,1)S(1)} copy-done((bf16[256,128]{1,0:T(8,128)(2,1)S(1)}, bf16[256,128]{1,0:T(8,128)(2,1)}, u32[]{:S(2)}) %copy-start.2) | copy-done | bytes 65560
  4.6 0.0 copy-start.3
  4.6 0.8 %copy-done.3 = bf16[256,128]{1,0:T(8,128)(2,1)S(1)} copy-done((bf16[256,128]{1,0:T(8,128)(2,1)S(1)}, bf16[256,128]{1,0:T(8,128)(2,1)}, u32[]{:S(2)}) %copy-start.3) | copy-done | bytes 65560
  5.4 0.0 copy-start.4
  5.4 0.7 copy-done.4
  6.2 67.6 %shard_map.102 = (bf16[256,128]{1,0:T(8,128)(2,1)S(1)}, bf16[256,128]{1,0:T(8,128)(2,1)S(1)}, f32[216,128]{1,0:T(8,128)S(1)}, f32[216,128]{1,0:T(8,128)S(1)}) custom-call(bf16[256,128]{1,0:T(8,128)(2,1)S(1)} %copy-done.2, s32[27,2,128]{2,1,0:T(2,128)S(1)} %copy-done.4, s32[27,2]{1,0:T(8,128)S(1)} %copy.11.codes, s32[1]{0:T(128)S(6)} %copy.16.count, ...), custom_call_target="tpu_custom_call" | custom-call | tf_op jit(solution)/shard_map/pallas_call | solution.py:456
  73.7 0.6 copy.17
  74.4 0.6 copy.18
  75.0 0.6 copy.19
  75.6 0.6 copy.20
Async XLA Ops:
  0.6 0.7 copy-start.5
  1.4 1.2 %copy-start = (bf16[27,128,128]{2,1,0:T(8,128)(2,1)S(1)}, bf16[27,128,128]{2,1,0:T(8,128)(2,1)}, u32[]{:S(2)}) copy-start(bf16[27,128,128]{2,1,0:T(8,128)(2,1)} %w_one.1) | copy-start | bytes 2654212
  2.6 1.2 %copy-start.1 = (bf16[27,128,128]{2,1,0:T(8,128)(2,1)S(1)}, bf16[27,128,128]{2,1,0:T(8,128)(2,1)}, u32[]{:S(2)}) copy-start(bf16[27,128,128]{2,1,0:T(8,128)(2,1)} %w_two.1) | copy-start | bytes 2654212
  3.7 0.8 %copy-start.2 = (bf16[256,128]{1,0:T(8,128)(2,1)S(1)}, bf16[256,128]{1,0:T(8,128)(2,1)}, u32[]{:S(2)}) copy-start(bf16[256,128]{1,0:T(8,128)(2,1)} %feat.1) | copy-start | bytes 196612
  4.6 0.8 %copy-start.3 = (bf16[256,128]{1,0:T(8,128)(2,1)S(1)}, bf16[256,128]{1,0:T(8,128)(2,1)}, u32[]{:S(2)}) copy-start(bf16[256,128]{1,0:T(8,128)(2,1)} %cot.1) | copy-start | bytes 196612
  5.4 0.7 copy-start.4

commit v2 on v1

--- a/solution.py
+++ b/solution.py
@@ -12,6 +12,7 @@
 BF = jnp.bfloat16
 F32 = jnp.float32
 I32 = jnp.int32
+UNROLL = 3
 
 
 def nn(a, b):
@@ -29,17 +30,22 @@
 
 def kernel(
     dims,
+    feat_hbm,
+    src_hbm,
+    codes_hbm,
+    count_hbm,
+    w_one,
+    w_two,
+    cot_hbm,
+    out_ref,
+    dx_ref,
+    wg_one,
+    wg_two,
     feat,
     src,
     codes,
     count,
-    w_one,
-    w_two,
     cot,
-    out_ref,
-    dx_ref,
-    wg_one,
-    wg_two,
     ot,
     pt,
     gt,
@@ -57,17 +63,25 @@
     cs,
     cr,
     sx,
-    rx,
+    sf,
+    r1,
+    r2,
+    r3,
+    s2,
+    r4,
     ab,
     bb,
     fb,
     w_sem,
+    i_sem,
     x_send,
     x_recv,
     c_send,
     c_recv,
     g_send,
     g_recv,
+    y_send,
+    y_recv,
     a_send,
     a_recv,
     b_send,
@@ -79,7 +93,7 @@
     third = kvol // 3
     B = rows_k
     shard = kvol * B // n_grp
-    half = cs.shape[2]
+    half = cs.shape[3]
     g = lax.axis_index("grp")
     t = lax.axis_index("tile")
     nz = n_tile // 2
@@ -93,9 +107,11 @@
     zlo = z % zside
     zhi = z // zside
 
-    def grp_of(o):
-        dy, dx = o // side, o % side
-        return lax.rem(gy + dy, side) * side + lax.rem(gx + dx, side)
+    def along(w, first, d):
+        y_axis = bool(w) == first
+        if y_axis:
+            return lax.rem(gy + d, side) * side + gx
+        return gy * side + lax.rem(gx + d, side)
 
     def near_z(d):
         return (zhi * zside + lax.rem(zlo + d, zside)) * 2 + core
@@ -103,17 +119,35 @@
     def far_z(d):
         return (lax.rem(zhi + d, zside) * zside + zlo) * 2 + core
 
+    inputs = [
+        pltpu.make_async_copy(a, b, i_sem.at[i])
+        for i, (a, b) in enumerate(
+            (
+                (src_hbm, src),
+                (codes_hbm, codes),
+                (count_hbm, count),
+                (feat_hbm, feat),
+                (cot_hbm, cot),
+            )
+        )
+    ]
+    for c in inputs[:4]:
+        c.start()
     for k, w in ((0, w_one), (1, w_two)):
         pltpu.make_async_copy(w, wraw.at[k], w_sem.at[k]).start()
+    inputs[4].start()
 
     barrier = pltpu.get_barrier_semaphore()
     partners = [{"tile": left}, {"tile": right}]
-    partners += [{"grp": grp_of(o)} for o in range(1, n_grp)]
+    partners += [{"grp": along(1, True, d)} for d in range(1, side)]
+    partners += [{"grp": along(0, True, d)} for d in range(1, side)]
     partners += [{"tile": near_z(d)} for d in range(1, zside)]
     partners += [{"tile": far_z(d)} for d in range(1, zside)]
     for p in partners:
         pl.semaphore_signal(barrier, inc=1, device_id=p, device_id_type=MESH)
 
+    for c in inputs[:4]:
+        c.wait()
     two = count[0] - 1
     two_f = two.astype(F32)
     one_f = 1.0 - two_f
@@ -123,12 +157,20 @@
     for j in range(2):
         ht[:, j * B : (j + 1) * B] = feat[j * B : (j + 1) * B, :].T
 
+    def sweep(body):
+        def several(i, carry):
+            for n in range(UNROLL):
+                body(i * UNROLL + n, carry)
+            return carry
+
+        lax.fori_loop(0, third // UNROLL, several, 0)
+
     iota = lax.broadcasted_iota(I32, (B, B), 0)
 
     def onehot(k, carry):
         for j in range(2):
             row = src[k, pl.ds(j, 1), :]
-            high = codes[k, j] & 1
+            high = codes[j, k] & 1
             live = two if j else 1
             for b in range(2):
                 m = (high if b else 1 - high) * live
@@ -150,7 +192,7 @@
                 wt[w, :, pl.ds(at, B)] = block.T
             return carry
 
-        lax.fori_loop(0, third, body, 0)
+        sweep(body)
 
     n1 = third * B
 
@@ -165,7 +207,7 @@
             put(4, i, nn(field[:, B:], ot[3 * i + 2, B:, :]))
             return carry
 
-        lax.fori_loop(0, third, body, 0)
+        sweep(body)
         to_prev = nn(wt[w, :, n1 : 2 * n1], pt[2 * n1 : 3 * n1, :])
         part_a = nn(wt[w, :, 2 * n1 :], pt[3 * n1 : 4 * n1, :])
         part_b = nn(wt[w, :, 2 * n1 :], pt[4 * n1 :, :])
@@ -179,7 +221,7 @@
             put(1, i, nn(field[:, B:], ot[3 * i, B:, :]))
             return carry
 
-        lax.fori_loop(0, third, body, 0)
+        sweep(body)
         return nn(wt[w, :, : 2 * n1], pt[: 2 * n1, :])
 
     def exchange(e, to_prev, to_next):
@@ -239,6 +281,7 @@
     moved = start(exchange(1, xs.at[1, 0], xs.at[1, 1]))
     pending += moved
     own = forward_own(hid, 1) + extra + ht[...].astype(F32)
+    inputs[4].wait()
     cot_t = jnp.concatenate(
         [cot[:B, :].astype(F32).T, cot[B:, :].astype(F32).T], axis=1
     )
@@ -263,7 +306,7 @@
             put_g(1, i, B, 2 * B, nt(q[w], ot[3 * i, B:, :]))
             return carry
 
-        lax.fori_loop(0, third, body, 0)
+        sweep(body)
 
     def back_edges(w, e):
         before, after = from_sides(e)
@@ -280,7 +323,7 @@
             put_g(2, i, B, 2 * B, nt(qe[2], ot[3 * i + 2, B:, :]))
             return carry
 
-        lax.fori_loop(0, third, body, 0)
+        sweep(body)
 
     def weight_grads(field, w):
         def body(i, carry):
@@ -290,58 +333,130 @@
                 wgf[w, pl.ds(to, B), :] = nt(field[...], gt[pl.ds(at, B), :])
             return carry
 
-        lax.fori_loop(0, third, body, 0)
-
-    def half_rows(w, s, h):
+        sweep(body)
+
+    def half_rows(w, rel, b, h):
+        a = lax.rem((gy if w else gx) + rel, side)
+        s = a * side + b if w else b * side + a
         at = pl.multiple_of(s * shard + h * half, 8)
         return wgf[w, pl.ds(at, half), :]
 
+    order = (2, 1, 3, 0)
+    spans = ((0, 1), (1, 3), (3, 4))
+
     def send_pair(w):
-        def body(s, carry):
-            cs[w, s] = half_rows(w, s, 1 - core).astype(BF)
-            return carry
-
-        lax.fori_loop(0, n_grp, body, 0)
+        copies = []
+        for n, (lo, hi) in enumerate(spans):
+            for p in range(lo, hi):
+
+                def body(b, carry, p=p):
+                    cs[w, p, b] = half_rows(w, order[p], b, 1 - core).astype(BF)
+                    return carry
+
+                lax.fori_loop(0, side, body, 0)
+            copies += start(
+                [
+                    pltpu.make_async_remote_copy(
+                        src_ref=cs.at[w, pl.ds(lo, hi - lo)],
+                        dst_ref=cr.at[w, pl.ds(lo, hi - lo)],
+                        send_sem=c_send.at[w, n],
+                        recv_sem=c_recv.at[w, n],
+                        device_id={"tile": sib},
+                        device_id_type=MESH,
+                    )
+                ]
+            )
+        return copies
+
+    def pair_sum(w, p):
+        def body(b, carry):
+            mine = half_rows(w, order[p], b, core)
+            sx[w, p, b] = (mine + cr[w, p, b].astype(F32)).astype(BF)
+            return carry
+
+        lax.fori_loop(0, side, body, 0)
+
+    mid = side // 2
+
+    def ring_copy(w, n, src_ref, dst_ref, d):
+        return pltpu.make_async_remote_copy(
+            src_ref=src_ref,
+            dst_ref=dst_ref,
+            send_sem=g_send.at[w, n],
+            recv_sem=g_recv.at[w, n],
+            device_id={"grp": along(w, True, d)},
+            device_id_type=MESH,
+        )
+
+    def ring_open(w, pair):
+        landed(pair[:1])
+        pair_sum(w, 0)
+        lo, hi = pl.ds(0, mid), pl.ds(mid, mid)
+        first = start(
+            [
+                ring_copy(w, 0, sx.at[w, 0, lo], r1.at[w, 0], 1),
+                ring_copy(w, 1, sx.at[w, 0, hi], r1.at[w, 1], side - 1),
+            ]
+        )
+        landed(pair[1:2])
+        pair_sum(w, 1)
+        pair_sum(w, 2)
+        second = start(
+            [
+                ring_copy(w, 2, sx.at[w, 1, hi], r2.at[w, 0], 1),
+                ring_copy(w, 3, sx.at[w, 2, lo], r2.at[w, 1], side - 1),
+            ]
+        )
+        return first, second
+
+    def ring_close(w, first):
+        landed(first)
+        third_leg = []
+        for n, (p, base, d) in enumerate(((1, 0, 1), (2, mid, side - 1))):
+
+            def body(b, carry, n=n, p=p, base=base):
+                v = sx[w, p, base + b].astype(F32) + r1[w, n, b].astype(F32)
+                sf[w, n, b] = v.astype(BF)
+                return carry
+
+            lax.fori_loop(0, mid, body, 0)
+            third_leg += start([ring_copy(w, 4 + n, sf.at[w, n], r3.at[w, n], d)])
+        return third_leg
+
+    def cross(w, pair, second, third_leg):
+        landed(pair[2:])
+        pair_sum(w, 3)
+        landed(second)
+        landed(third_leg)
+        for n in range(2):
+
+            def body(b, carry, n=n):
+                v = sx[w, 3, n * mid + b].astype(F32)
+                v = v + r3[w, n, b].astype(F32) + r2[w, 1 - n, b].astype(F32)
+                s2[w, n * mid + b] = v.astype(BF)
+                return carry
+
+            lax.fori_loop(0, mid, body, 0)
+        here = gx if w else gy
         return start(
             [
                 pltpu.make_async_remote_copy(
-                    src_ref=cs.at[w],
-                    dst_ref=cr.at[w],
-                    send_sem=c_send.at[w],
-                    recv_sem=c_recv.at[w],
-                    device_id={"tile": sib},
+                    src_ref=s2.at[w, lax.rem(here + d, side)],
+                    dst_ref=r4.at[w, d],
+                    send_sem=y_send.at[w, d],
+                    recv_sem=y_recv.at[w, d],
+                    device_id={"grp": along(w, False, d)},
                     device_id_type=MESH,
                 )
-            ]
-        )
-
-    def send_plane(w, moved):
-        landed(moved)
-
-        def body(s, carry):
-            sx[w, s] = (half_rows(w, s, core) + cr[w, s].astype(F32)).astype(BF)
-            return carry
-
-        lax.fori_loop(0, n_grp, body, 0)
-        return start(
-            [
-                pltpu.make_async_remote_copy(
-                    src_ref=sx.at[w, grp_of(o)],
-                    dst_ref=rx.at[w, o],
-                    send_sem=g_send.at[w, o],
-                    recv_sem=g_recv.at[w, o],
-                    device_id={"grp": grp_of(o)},
-                    device_id_type=MESH,
-                )
-                for o in range(1, n_grp)
+                for d in range(1, side)
             ]
         )
 
     def send_near(w, moved):
         landed(moved)
-        acc = sx[w, g].astype(F32)
-        for o in range(1, n_grp):
-            acc = acc + rx[w, o].astype(F32)
+        acc = s2[w, gx if w else gy].astype(F32)
+        for d in range(1, side):
+            acc = acc + r4[w, d].astype(F32)
         ab[w, zlo] = acc.astype(BF)
         return start(
             [
@@ -418,27 +533,43 @@
     weight_grads(hid, 1)
     pair_two = send_pair(1)
     back_own(0)
-    plane_two = send_plane(1, pair_two)
+    first_two, second_two = ring_open(1, pair_two)
     landed(moved)
     back_edges(0, 3)
     weight_grads(ht, 0)
     pair_one = send_pair(0)
+    third_two = ring_close(1, first_two)
+    first_one, second_one = ring_open(0, pair_one)
+    cross_two = cross(1, pair_two, second_two, third_two)
+    third_one = ring_close(0, first_one)
     grad_in = nn(wc[0], gt[...]) + q[1].astype(F32)
-    plane_one = send_plane(0, pair_one)
+    cross_one = cross(0, pair_one, second_one, third_one)
+    near_two = send_near(1, cross_two)
     for j in range(2):
         dx_ref[j * B : (j + 1) * B, :] = grad_in[:, j * B : (j + 1) * B].T.astype(BF)
-    near_two = send_near(1, plane_two)
-    near_one = send_near(0, plane_one)
+    near_one = send_near(0, cross_one)
     far_two = send_far(1, near_two)
     far_one = send_far(0, near_one)
     last_two = send_last(1, far_two)
     finish(1, last_two)
     last_one = send_last(0, far_one)
     finish(0, last_one)
-    pending += pair_two + plane_two + pair_one + plane_one
-    pending += near_two + near_one + far_two + far_one + last_two + last_one
+    for w in (pair_two, first_two, second_two, third_two, cross_two, near_two):
+        pending += w
+    for w in (pair_one, first_one, second_one, third_one, cross_one, near_one):
+        pending += w
+    pending += far_two + far_one + last_two + last_one
     for c in pending:
         c.wait_send()
+
+
+def settle(*refs):
+    sem = refs[8]
+    copies = [pltpu.make_async_copy(refs[i], refs[4 + i], sem.at[i]) for i in range(4)]
+    for c in copies:
+        c.start()
+    for c in copies:
+        c.wait()
 
 
 def on_device(n_grp, n_tile, features, source_rows, target_codes, block_count, w1, w2, cot):
@@ -449,11 +580,10 @@
     half = -(-shard // 32) * 16
     wide = kvol * B
     vmem = pl.BlockSpec(memory_space=pltpu.VMEM)
-    smem = pl.BlockSpec(memory_space=pltpu.SMEM)
-    hbm = pl.BlockSpec(memory_space=pl.ANY)
+    hbm = pl.BlockSpec(memory_space=pltpu.HBM)
     dma = pltpu.SemaphoreType.DMA
     dims = (n_grp, n_tile, kvol, B, side, zside)
-    return pl.pallas_call(
+    results = pl.pallas_call(
         functools.partial(kernel, dims),
         out_shape=(
             jax.ShapeDtypeStruct((2 * B, B), BF),
@@ -461,9 +591,14 @@
             jax.ShapeDtypeStruct((shard, B), F32),
             jax.ShapeDtypeStruct((shard, B), F32),
         ),
-        in_specs=[vmem, vmem, smem, smem, hbm, hbm, vmem],
+        in_specs=[hbm] * 7,
         out_specs=(vmem,) * 4,
         scratch_shapes=[
+            pltpu.VMEM((2 * B, B), BF),
+            pltpu.VMEM((kvol, 2, B), I32),
+            pltpu.SMEM((2, kvol), I32),
+            pltpu.SMEM((1,), I32),
+            pltpu.VMEM((2 * B, B), BF),
             pltpu.VMEM((kvol, 2 * B, 2 * B), BF),
             pltpu.VMEM((5 * (kvol // 3) * B, 2 * B), BF),
             pltpu.VMEM((wide, 2 * B), BF),
@@ -478,20 +613,28 @@
             pltpu.VMEM((4, 2, B, 2 * B), BF),
             pltpu.VMEM((3, B, 2 * B), BF),
             pltpu.VMEM((2, wide + 2 * half - shard, B), F32),
-            pltpu.VMEM((2, n_grp, half, B), BF),
-            pltpu.VMEM((2, n_grp, half, B), BF),
-            pltpu.VMEM((2, n_grp, half, B), BF),
-            pltpu.VMEM((2, n_grp, half, B), BF),
+            pltpu.VMEM((2, side, side, half, B), BF),
+            pltpu.VMEM((2, side, side, half, B), BF),
+            pltpu.VMEM((2, side, side, half, B), BF),
+            pltpu.VMEM((2, 2, side // 2, half, B), BF),
+            pltpu.VMEM((2, 2, side // 2, half, B), BF),
+            pltpu.VMEM((2, 2, side // 2, half, B), BF),
+            pltpu.VMEM((2, 2, side // 2, half, B), BF),
+            pltpu.VMEM((2, side, half, B), BF),
+            pltpu.VMEM((2, side, half, B), BF),
             pltpu.VMEM((2, zside, half, B), BF),
             pltpu.VMEM((2, zside, half, B), BF),
             pltpu.VMEM((2, 2, half, B), F32),
             dma((2,)),
+            dma((5,)),
             dma((4, 2)),
             dma((4, 2)),
-            dma((2,)),
-            dma((2,)),
-            dma((2, n_grp)),
-            dma((2, n_grp)),
+            dma((2, 3)),
+            dma((2, 3)),
+            dma((2, 6)),
+            dma((2, 6)),
+            dma((2, side)),
+            dma((2, side)),
             dma((2, zside)),
             dma((2, zside)),
             dma((2, zside)),
@@ -500,9 +643,16 @@
             dma((2,)),
         ],
         compiler_params=pltpu.CompilerParams(
-            collective_id=0, has_side_effects=True, vmem_limit_bytes=48 * 1024 * 1024
+            collective_id=0, has_side_effects=True, vmem_limit_bytes=67043328
         ),
-    )(features, source_rows, target_codes, block_count, w1, w2, cot)
+    )(features, source_rows, target_codes.T, block_count, w1, w2, cot)
+    return pl.pallas_call(
+        settle,
+        out_shape=tuple(jax.ShapeDtypeStruct(r.shape, r.dtype) for r in results),
+        in_specs=[vmem] * 4,
+        out_specs=(hbm,) * 4,
+        scratch_shapes=[dma((4,))],
+    )(*results)
 
 
 def solution(mesh):

time: 76.7 us -> 67.9 us (0.89)
  local copies, waits for them, and re-layouts: 7.42 us -> 0 us
  Pallas kernels: 67.6 us -> 66.5 us
    unnamed x17 -> x0, local copies, waits for them, and re-layouts: 7.42 us -> none
    pallas_call x1, Pallas kernels: 67.6 us -> 64.7 us  [on_device(): pl.pallas_call(functools.partial(kernel, dims), out_shape=(jax.ShapeDtype...]
    pallas_call x0 -> x1, Pallas kernels: none -> 1.78 us  [on_device(): pl.pallas_call(settle, out_shape=tuple((jax.ShapeDtypeStruct(r.shape, r.d...]
where the time goes in v2:
time: 67.9 us; the launch traced here: 67.8 us
  Pallas kernels  66.5 us (98%)
  between operations  1.29 us (2%)
    pallas_call x1, Pallas kernels, on_device(): pl.pallas_call(functools.partial(kernel, dims), out_shape=(jax.ShapeDtype...  64.7 us
    pallas_call x1, Pallas kernels, on_device(): pl.pallas_call(settle, out_shape=tuple((jax.ShapeDtypeStruct(r.shape, r.d...  1.78 us

profile of v2, /device:TPU:1, one launch (start us, length us, event | category | flops | bytes accessed | tf_op | source)
XLA Modules:
  0.0 67.8 jit_solution(9802659369494285850)
XLA Ops:
  1.3 64.7 %shard_map.102 = (bf16[256,128]{1,0:T(8,128)(2,1)}, bf16[256,128]{1,0:T(8,128)(2,1)}, f32[216,128]{1,0:T(8,128)}, f32[216,128]{1,0:T(8,128)}) custom-call(bf16[256,128]{1,0:T(8,128)(2,1)} %feat_hbm.1, s32[27,2,128]{2,1,0:T(2,128)} %src_hbm.1, s32[2,27]{1,0:T(2,128)} %bitcast.1, s32[1]{0:T(128)S(6)} %copy.11.count_hbm, bf16[27,128,128]{2,1,0:T(8,128)(2,1)} %w_one.1, ...), custom_call_target="tpu_custom_call" | custom-call | tf_op jit(solution)/shard_map/pallas_call | solution.py:586
  66.0 1.8 %shard_map.103 = (bf16[256,128]{1,0:T(8,128)(2,1)}, bf16[256,128]{1,0:T(8,128)(2,1)}, f32[216,128]{1,0:T(8,128)}, f32[216,128]{1,0:T(8,128)}) custom-call(bf16[256,128]{1,0:T(8,128)(2,1)} %get-tuple-element.8.refs_0_, bf16[256,128]{1,0:T(8,128)(2,1)} %get-tuple-element.9.refs_1_, f32[216,128]{1,0:T(8,128)} %get-tuple-element.10.refs_2_, ...), custom_call_target="tpu_custom_call" | custom-call | tf_op jit(solution)/shard_map/pallas_call | solution.py:649

commit v3 on v2

--- a/solution.py
+++ b/solution.py
@@ -12,7 +12,7 @@
 BF = jnp.bfloat16
 F32 = jnp.float32
 I32 = jnp.int32
-UNROLL = 3
+UNROLL = 9
 
 
 def nn(a, b):
@@ -59,6 +59,7 @@
     xs,
     xr,
     qe,
+    hl,
     wgf,
     cs,
     cr,
@@ -107,11 +108,10 @@
     zlo = z % zside
     zhi = z // zside
 
-    def along(w, first, d):
-        y_axis = bool(w) == first
-        if y_axis:
-            return lax.rem(gy + d, side) * side + gx
-        return gy * side + lax.rem(gx + d, side)
+    def along(axis, d):
+        if axis:
+            return gy * side + lax.rem(gx + d, side)
+        return lax.rem(gy + d, side) * side + gx
 
     def near_z(d):
         return (zhi * zside + lax.rem(zlo + d, zside)) * 2 + core
@@ -139,8 +139,7 @@
 
     barrier = pltpu.get_barrier_semaphore()
     partners = [{"tile": left}, {"tile": right}]
-    partners += [{"grp": along(1, True, d)} for d in range(1, side)]
-    partners += [{"grp": along(0, True, d)} for d in range(1, side)]
+    partners += [{"grp": along(axis, d)} for axis in range(2) for d in range(1, side)]
     partners += [{"tile": near_z(d)} for d in range(1, zside)]
     partners += [{"tile": far_z(d)} for d in range(1, zside)]
     for p in partners:
@@ -167,32 +166,58 @@
 
     iota = lax.broadcasted_iota(I32, (B, B), 0)
 
-    def onehot(k, carry):
+    def fill(k, at, row, high, live):
+        for b in range(2):
+            m = (high if b else 1 - high) * live
+            idx = row * m + (m - 1)
+            hit = jnp.where(iota == idx, 1.0, 0.0).astype(BF)
+            ot[k, at : at + B, b * B : (b + 1) * B] = hit
+
+    def entry(k, j):
+        return src[k, pl.ds(j, 1), :], codes[j, k] & 1
+
+    def fill_edges(i, carry):
+        row, high = entry(3 * i, 0)
+        fill(3 * i, 0, row, high, 1)
+        k = 3 * i + 2
+        row, high = entry(k, 0)
+        row_b, high_b = entry(k, 1)
+        row = row * (1 - two) + row_b * two
+        high = high * (1 - two) + high_b * two
+        fill(k, B, row, high, 1)
+
+    def fill_own(i, carry):
+        k = 3 * i + 1
         for j in range(2):
-            row = src[k, pl.ds(j, 1), :]
-            high = codes[j, k] & 1
-            live = two if j else 1
-            for b in range(2):
-                m = (high if b else 1 - high) * live
-                idx = row * m + (m - 1)
-                hit = jnp.where(iota == idx, 1.0, 0.0).astype(BF)
-                ot[k, j * B : (j + 1) * B, b * B : (b + 1) * B] = hit
-        return carry
-
-    lax.fori_loop(0, kvol, onehot, 0)
-
-    def prep(w):
+            row, high = entry(k, j)
+            fill(k, j * B, row, high, two if j else 1)
+        row, high = entry(3 * i, 1)
+        fill(3 * i, B, row, high, two)
+        row, high = entry(3 * i + 2, 0)
+        fill(3 * i + 2, 0, row, high, two)
+
+    sweep(fill_edges)
+
+    slots = {1: 0, 0: 1, 2: 2}
+
+    def prep_t(w, classes):
+        def body(i, carry):
+            for cls in classes:
+                at = pl.multiple_of((slots[cls] * third + i) * B, B)
+                wt[w, :, pl.ds(at, B)] = wraw[w, 3 * i + cls].T
+
+        sweep(body)
+
+    def prep_c(w):
+        def body(i, carry):
+            for cls in range(3):
+                at = pl.multiple_of((slots[cls] * third + i) * B, B)
+                wc[w, :, pl.ds(at, B)] = wraw[w, 3 * i + cls]
+
+        sweep(body)
+
+    def weights_here(w):
         pltpu.make_async_copy(w_two if w else w_one, wraw.at[w], w_sem.at[w]).wait()
-
-        def body(i, carry):
-            for pos, cls in enumerate((1, 0, 2)):
-                at = pl.multiple_of((pos * third + i) * B, B)
-                block = wraw[w, 3 * i + cls]
-                wc[w, :, pl.ds(at, B)] = block
-                wt[w, :, pl.ds(at, B)] = block.T
-            return carry
-
-        sweep(body)
 
     n1 = third * B
 
@@ -201,28 +226,27 @@
         pt[pl.ds(at, B), :] = value.astype(BF)
 
     def forward_edges(field, w):
+        v = field[:, :B].astype(F32) * one_f + field[:, B:].astype(F32) * two_f
+        hl[...] = v.astype(BF)
+
         def body(i, carry):
-            put(2, i, nn(field[:, :B], ot[3 * i, :B, :]))
-            put(3, i, nn(field[:, :B], ot[3 * i + 2, :B, :]))
-            put(4, i, nn(field[:, B:], ot[3 * i + 2, B:, :]))
-            return carry
+            put(3, i, nn(field[:, :B], ot[3 * i, :B, :]))
+            put(4, i, nn(hl[...], ot[3 * i + 2, B:, :]))
 
         sweep(body)
-        to_prev = nn(wt[w, :, n1 : 2 * n1], pt[2 * n1 : 3 * n1, :])
-        part_a = nn(wt[w, :, 2 * n1 :], pt[3 * n1 : 4 * n1, :])
-        part_b = nn(wt[w, :, 2 * n1 :], pt[4 * n1 :, :])
+        to_prev = nn(wt[w, :, n1 : 2 * n1], pt[3 * n1 : 4 * n1, :])
+        to_next = nn(wt[w, :, 2 * n1 :], pt[4 * n1 :, :])
         xs[w, 0] = to_prev.astype(BF)
-        xs[w, 1] = (part_b + part_a * one_f).astype(BF)
-        return part_a * two_f
+        xs[w, 1] = to_next.astype(BF)
 
     def forward_own(field, w):
         def body(i, carry):
             put(0, i, nn(field[...], ot[3 * i + 1]))
             put(1, i, nn(field[:, B:], ot[3 * i, B:, :]))
-            return carry
+            put(2, i, nn(field[:, :B], ot[3 * i + 2, :B, :]))
 
         sweep(body)
-        return nn(wt[w, :, : 2 * n1], pt[: 2 * n1, :])
+        return nn(wt[w], pt[: 3 * n1, :])
 
     def exchange(e, to_prev, to_next):
         return [
@@ -264,23 +288,28 @@
         lax.broadcasted_iota(I32, (1, 2 * B), 1) < B * count[0], 1.0, 0.0
     )
 
-    prep(0)
-    extra = forward_edges(ht, 0)
+    weights_here(0)
+    prep_t(0, (0, 2))
+    forward_edges(ht, 0)
     pl.semaphore_wait(barrier, len(partners))
     moved = start(exchange(0, xs.at[0, 0], xs.at[0, 1]))
     pending += moved
-    own = forward_own(ht, 0) + extra
-    prep(1)
+    sweep(fill_own)
+    prep_t(0, (1,))
+    own = forward_own(ht, 0)
+    weights_here(1)
+    prep_t(1, (0, 1, 2))
     landed(moved)
     before, after = from_sides(0)
     pre_one = own + before + after
     pre[...] = pre_one
     hid[...] = (silu_parts(pre_one)[0] * mask).astype(BF)
 
-    extra = forward_edges(hid, 1)
+    forward_edges(hid, 1)
     moved = start(exchange(1, xs.at[1, 0], xs.at[1, 1]))
     pending += moved
-    own = forward_own(hid, 1) + extra + ht[...].astype(F32)
+    own = forward_own(hid, 1) + ht[...].astype(F32)
+    prep_c(1)
     inputs[4].wait()
     cot_t = jnp.concatenate(
         [cot[:B, :].astype(F32).T, cot[B:, :].astype(F32).T], axis=1
@@ -304,42 +333,42 @@
         def body(i, carry):
             put_g(0, i, 0, 2 * B, nt(q[w], ot[3 * i + 1]))
             put_g(1, i, B, 2 * B, nt(q[w], ot[3 * i, B:, :]))
-            return carry
+            put_g(2, i, 0, B, nt(q[w], ot[3 * i + 2, :B, :]))
 
         sweep(body)
 
     def back_edges(w, e):
         before, after = from_sides(e)
-        mixed = (after * one_f + q[w].astype(F32) * two_f).astype(BF)
-        before = before.astype(BF)
-        after = after.astype(BF)
-        qe[0] = before
-        qe[1] = mixed
-        qe[2] = after
+        qe[0] = before.astype(BF)
+        qe[1] = after.astype(BF)
 
         def body(i, carry):
             put_g(1, i, 0, B, nt(qe[0], ot[3 * i, :B, :]))
-            put_g(2, i, 0, B, nt(qe[1], ot[3 * i + 2, :B, :]))
-            put_g(2, i, B, 2 * B, nt(qe[2], ot[3 * i + 2, B:, :]))
-            return carry
+            last = nt(qe[1], ot[3 * i + 2, B:, :])
+            at = pl.multiple_of((2 * third + i) * B, B)
+            lower = gt[pl.ds(at, B), :B].astype(F32)
+            put_g(2, i, 0, B, lower + last * one_f)
+            put_g(2, i, B, 2 * B, last * two_f)
 
         sweep(body)
 
-    def weight_grads(field, w):
+    def weight_grads(field, w, classes):
         def body(i, carry):
-            for pos, cls in enumerate((1, 0, 2)):
-                at = pl.multiple_of((pos * third + i) * B, B)
+            for cls in classes:
+                at = pl.multiple_of((slots[cls] * third + i) * B, B)
                 to = pl.multiple_of((3 * i + cls) * B, B)
                 wgf[w, pl.ds(to, B), :] = nt(field[...], gt[pl.ds(at, B), :])
-            return carry
 
         sweep(body)
 
-    def half_rows(w, rel, b, h):
-        a = lax.rem((gy if w else gx) + rel, side)
-        s = a * side + b if w else b * side + a
-        at = pl.multiple_of(s * shard + h * half, 8)
-        return wgf[w, pl.ds(at, half), :]
+    cut = -(-half // 32) * 16
+    rows = (pl.ds(0, cut), pl.ds(cut, half - cut))
+
+    def half_rows(w, r, rel, b, h):
+        a = lax.rem((gx if r else gy) + rel, side)
+        s = b * side + a if r else a * side + b
+        at = pl.multiple_of(s * shard + h * half + rows[r].start, 8)
+        return wgf[w, pl.ds(at, rows[r].size), :]
 
     order = (2, 1, 3, 0)
     spans = ((0, 1), (1, 3), (3, 4))
@@ -350,7 +379,9 @@
             for p in range(lo, hi):
 
                 def body(b, carry, p=p):
-                    cs[w, p, b] = half_rows(w, order[p], b, 1 - core).astype(BF)
+                    for r in range(2):
+                        v = half_rows(w, r, order[p], b, 1 - core)
+                        cs[w, p, b, rows[r]] = v.astype(BF)
                     return carry
 
                 lax.fori_loop(0, side, body, 0)
@@ -370,43 +401,48 @@
 
     def pair_sum(w, p):
         def body(b, carry):
-            mine = half_rows(w, order[p], b, core)
-            sx[w, p, b] = (mine + cr[w, p, b].astype(F32)).astype(BF)
+            for r in range(2):
+                v = half_rows(w, r, order[p], b, core)
+                v = v + cr[w, p, b, rows[r]].astype(F32)
+                sx[w, p, b, rows[r]] = v.astype(BF)
             return carry
 
         lax.fori_loop(0, side, body, 0)
 
     mid = side // 2
-
-    def ring_copy(w, n, src_ref, dst_ref, d):
+    low, top = pl.ds(0, mid), pl.ds(mid, mid)
+
+    def ring_copy(w, r, n, src_ref, dst_ref, d):
         return pltpu.make_async_remote_copy(
-            src_ref=src_ref,
-            dst_ref=dst_ref,
-            send_sem=g_send.at[w, n],
-            recv_sem=g_recv.at[w, n],
-            device_id={"grp": along(w, True, d)},
+            src_ref=src_ref.at[:, rows[r]],
+            dst_ref=dst_ref.at[:, rows[r]],
+            send_sem=g_send.at[w, r, n],
+            recv_sem=g_recv.at[w, r, n],
+            device_id={"grp": along(r, d)},
             device_id_type=MESH,
         )
 
     def ring_open(w, pair):
         landed(pair[:1])
         pair_sum(w, 0)
-        lo, hi = pl.ds(0, mid), pl.ds(mid, mid)
-        first = start(
-            [
-                ring_copy(w, 0, sx.at[w, 0, lo], r1.at[w, 0], 1),
-                ring_copy(w, 1, sx.at[w, 0, hi], r1.at[w, 1], side - 1),
-            ]
-        )
+        first, second = [], []
+        for r in range(2):
+            first += start(
+                [
+                    ring_copy(w, r, 0, sx.at[w, 0, low], r1.at[w, 0], 1),
+                    ring_copy(w, r, 1, sx.at[w, 0, top], r1.at[w, 1], side - 1),
+                ]
+            )
         landed(pair[1:2])
         pair_sum(w, 1)
         pair_sum(w, 2)
-        second = start(
-            [
-                ring_copy(w, 2, sx.at[w, 1, hi], r2.at[w, 0], 1),
-                ring_copy(w, 3, sx.at[w, 2, lo], r2.at[w, 1], side - 1),
-            ]
-        )
+        for r in range(2):
+            second += start(
+                [
+                    ring_copy(w, r, 2, sx.at[w, 1, top], r2.at[w, 0], 1),
+                    ring_copy(w, r, 3, sx.at[w, 2, low], r2.at[w, 1], side - 1),
+                ]
+            )
         return first, second
 
     def ring_close(w, first):
@@ -420,7 +456,10 @@
                 return carry
 
             lax.fori_loop(0, mid, body, 0)
-            third_leg += start([ring_copy(w, 4 + n, sf.at[w, n], r3.at[w, n], d)])
+            for r in range(2):
+                third_leg += start(
+                    [ring_copy(w, r, 4 + n, sf.at[w, n], r3.at[w, n], d)]
+                )
         return third_leg
 
     def cross(w, pair, second, third_leg):
@@ -437,27 +476,28 @@
                 return carry
 
             lax.fori_loop(0, mid, body, 0)
-        here = gx if w else gy
         return start(
             [
                 pltpu.make_async_remote_copy(
-                    src_ref=s2.at[w, lax.rem(here + d, side)],
-                    dst_ref=r4.at[w, d],
-                    send_sem=y_send.at[w, d],
-                    recv_sem=y_recv.at[w, d],
-                    device_id={"grp": along(w, False, d)},
+                    src_ref=s2.at[w, lax.rem((gy if r else gx) + d, side), rows[r]],
+                    dst_ref=r4.at[w, d, rows[r]],
+                    send_sem=y_send.at[w, r, d],
+                    recv_sem=y_recv.at[w, r, d],
+                    device_id={"grp": along(1 - r, d)},
                     device_id_type=MESH,
                 )
-                for d in range(1, side)
+                for d in (2, 1, 3)
+                for r in range(2)
             ]
         )
 
     def send_near(w, moved):
         landed(moved)
-        acc = s2[w, gx if w else gy].astype(F32)
-        for d in range(1, side):
-            acc = acc + r4[w, d].astype(F32)
-        ab[w, zlo] = acc.astype(BF)
+        for r in range(2):
+            acc = s2[w, gy if r else gx, rows[r]].astype(F32)
+            for d in range(1, side):
+                acc = acc + r4[w, d, rows[r]].astype(F32)
+            ab[w, zlo, rows[r]] = acc.astype(BF)
         return start(
             [
                 pltpu.make_async_remote_copy(
@@ -530,18 +570,20 @@
     q[0] = (grad_mid * slope * mask).astype(BF)
     moved = start(exchange(3, q.at[0], q.at[0]))
     pending += moved
-    weight_grads(hid, 1)
+    weight_grads(hid, 1, (0, 1, 2))
     pair_two = send_pair(1)
     back_own(0)
+    weight_grads(ht, 0, (1,))
     first_two, second_two = ring_open(1, pair_two)
     landed(moved)
     back_edges(0, 3)
-    weight_grads(ht, 0)
+    weight_grads(ht, 0, (0, 2))
     pair_one = send_pair(0)
     third_two = ring_close(1, first_two)
     first_one, second_one = ring_open(0, pair_one)
     cross_two = cross(1, pair_two, second_two, third_two)
     third_one = ring_close(0, first_one)
+    prep_c(0)
     grad_in = nn(wc[0], gt[...]) + q[1].astype(F32)
     cross_one = cross(0, pair_one, second_one, third_one)
     near_two = send_near(1, cross_two)
@@ -611,7 +653,8 @@
             pltpu.VMEM((2, B, 2 * B), BF),
             pltpu.VMEM((2, 2, B, 2 * B), BF),
             pltpu.VMEM((4, 2, B, 2 * B), BF),
-            pltpu.VMEM((3, B, 2 * B), BF),
+            pltpu.VMEM((2, B, 2 * B), BF),
+            pltpu.VMEM((B, B), BF),
             pltpu.VMEM((2, wide + 2 * half - shard, B), F32),
             pltpu.VMEM((2, side, side, half, B), BF),
             pltpu.VMEM((2, side, side, half, B), BF),
@@ -631,10 +674,10 @@
             dma((4, 2)),
             dma((2, 3)),
             dma((2, 3)),
-            dma((2, 6)),
-            dma((2, 6)),
-            dma((2, side)),
-            dma((2, side)),
+            dma((2, 2, 6)),
+            dma((2, 2, 6)),
+            dma((2, 2, side)),
+            dma((2, 2, side)),
             dma((2, zside)),
             dma((2, zside)),
             dma((2, zside)),

time: 67.9 us -> 66 us (0.972)
  Pallas kernels: 66.5 us -> 64.6 us
    pallas_call x1, Pallas kernels: 64.7 us -> 62.8 us  [on_device(): pl.pallas_call(functools.partial(kernel, dims), out_shape=(jax.ShapeDtype...]
where the time goes in v3:
time: 66 us; the launch traced here: 65.8 us
  Pallas kernels  64.6 us (98%)
  between operations  1.29 us (2%)
    pallas_call x1, Pallas kernels, on_device(): pl.pallas_call(functools.partial(kernel, dims), out_shape=(jax.ShapeDtype...  62.8 us
    pallas_call x1, Pallas kernels, on_device(): pl.pallas_call(settle, out_shape=tuple((jax.ShapeDtypeStruct(r.shape, r.d...  1.78 us

profile of v3, /device:TPU:1, one launch (start us, length us, event | category | flops | bytes accessed | tf_op | source)
XLA Modules:
  0.0 65.8 jit_solution(1705722460886365865)
XLA Ops:
  1.3 62.8 %shard_map.102 = (bf16[256,128]{1,0:T(8,128)(2,1)}, bf16[256,128]{1,0:T(8,128)(2,1)}, f32[216,128]{1,0:T(8,128)}, f32[216,128]{1,0:T(8,128)}) custom-call(bf16[256,128]{1,0:T(8,128)(2,1)} %feat_hbm.1, s32[27,2,128]{2,1,0:T(2,128)} %src_hbm.1, s32[2,27]{1,0:T(2,128)} %bitcast.1, s32[1]{0:T(128)S(6)} %copy.11.count_hbm, bf16[27,128,128]{2,1,0:T(8,128)(2,1)} %w_one.1, ...), custom_call_target="tpu_custom_call" | custom-call | tf_op jit(solution)/shard_map/pallas_call | solution.py:628
  64.1 1.8 %shard_map.103 = (bf16[256,128]{1,0:T(8,128)(2,1)}, bf16[256,128]{1,0:T(8,128)(2,1)}, f32[216,128]{1,0:T(8,128)}, f32[216,128]{1,0:T(8,128)}) custom-call(bf16[256,128]{1,0:T(8,128)(2,1)} %get-tuple-element.8.refs_0_, bf16[256,128]{1,0:T(8,128)(2,1)} %get-tuple-element.9.refs_1_, f32[216,128]{1,0:T(8,128)} %get-tuple-element.10.refs_2_, ...), custom_call_target="tpu_custom_call" | custom-call | tf_op jit(solution)/shard_map/pallas_call | solution.py:692

commit v4 on v3

--- a/solution.py
+++ b/solution.py
@@ -625,6 +625,9 @@
     hbm = pl.BlockSpec(memory_space=pltpu.HBM)
     dma = pltpu.SemaphoreType.DMA
     dims = (n_grp, n_tile, kvol, B, side, zside)
+    held = functools.partial(
+        pltpu.with_memory_space_constraint, memory_space=pltpu.HBM
+    )
     results = pl.pallas_call(
         functools.partial(kernel, dims),
         out_shape=(
@@ -686,15 +689,24 @@
             dma((2,)),
         ],
         compiler_params=pltpu.CompilerParams(
-            collective_id=0, has_side_effects=True, vmem_limit_bytes=67043328
+            collective_id=0, has_side_effects=True, vmem_limit_bytes=48 * 1024 * 1024
         ),
-    )(features, source_rows, target_codes.T, block_count, w1, w2, cot)
+    )(
+        held(features),
+        held(source_rows),
+        held(target_codes.T),
+        block_count,
+        held(w1),
+        held(w2),
+        held(cot),
+    )
     return pl.pallas_call(
         settle,
         out_shape=tuple(jax.ShapeDtypeStruct(r.shape, r.dtype) for r in results),
         in_specs=[vmem] * 4,
         out_specs=(hbm,) * 4,
         scratch_shapes=[dma((4,))],
+        compiler_params=pltpu.CompilerParams(vmem_limit_bytes=4 * 1024 * 1024),
     )(*results)
 
 

time: 66 us -> 64.3 us (0.974)
  Pallas kernels: 64.6 us -> 62.8 us
    pallas_call x1, Pallas kernels: 1.78 us -> 0.76 us  [on_device(): pl.pallas_call(settle, out_shape=tuple((jax.ShapeDtypeStruct(r.shape, r.d...]
    pallas_call x1, Pallas kernels: 62.8 us -> 62.1 us  [on_device(): pl.pallas_call(functools.partial(kernel, dims), out_shape=(jax.ShapeDtype...]
where the time goes in v4:
time: 64.3 us; the launch traced here: 64.1 us
  Pallas kernels  62.8 us (98%)
  between operations  1.29 us (2%)
    pallas_call x1, Pallas kernels, on_device(): pl.pallas_call(functools.partial(kernel, dims), out_shape=(jax.ShapeDtype...  62.1 us

profile of v4, /device:TPU:1, one launch (start us, length us, event | category | flops | bytes accessed | tf_op | source)
XLA Modules:
  0.0 64.1 jit_solution(4118537434317998271)
XLA Ops:
  1.3 62.1 %shard_map.102 = (bf16[256,128]{1,0:T(8,128)(2,1)S(1)}, bf16[256,128]{1,0:T(8,128)(2,1)S(1)}, f32[216,128]{1,0:T(8,128)S(1)}, f32[216,128]{1,0:T(8,128)S(1)}) custom-call(bf16[256,128]{1,0:T(8,128)(2,1)} %feat_hbm.1, s32[27,2,128]{2,1,0:T(2,128)} %src_hbm.1, s32[2,27]{1,0:T(2,128)} %bitcast.1, s32[1]{0:T(128)S(6)} %copy.11.count_hbm, ...), custom_call_target="tpu_custom_call" | custom-call | tf_op jit(solution)/shard_map/pallas_call | solution.py:631
  63.3 0.8 %shard_map.103 = (bf16[256,128]{1,0:T(8,128)(2,1)}, bf16[256,128]{1,0:T(8,128)(2,1)}, f32[216,128]{1,0:T(8,128)}, f32[216,128]{1,0:T(8,128)}) custom-call(bf16[256,128]{1,0:T(8,128)(2,1)S(1)} %get-tuple-element.8.refs_0_, bf16[256,128]{1,0:T(8,128)(2,1)S(1)} %get-tuple-element.9.refs_1_, f32[216,128]{1,0:T(8,128)S(1)} %get-tuple-element.10.refs_2_, ...), custom_call_target="tpu_custom_call" | custom-call | tf_op jit(solution)/shard_map/pallas_call | solution.py:703

commit v5 on v4

--- a/solution.py
+++ b/solution.py
@@ -89,6 +89,7 @@
     b_recv,
     f_send,
     f_recv,
+    hello,
 ):
     n_grp, n_tile, kvol, rows_k, side, zside = dims
     third = kvol // 3
@@ -139,14 +140,25 @@
 
     barrier = pltpu.get_barrier_semaphore()
     partners = [{"tile": left}, {"tile": right}]
-    partners += [{"grp": along(axis, d)} for axis in range(2) for d in range(1, side)]
-    partners += [{"tile": near_z(d)} for d in range(1, zside)]
-    partners += [{"tile": far_z(d)} for d in range(1, zside)]
+    beside = [{"grp": along(axis, d)} for axis in range(2) for d in (1, side - 1)]
+    partners += beside
     for p in partners:
         pl.semaphore_signal(barrier, inc=1, device_id=p, device_id_type=MESH)
 
     for c in inputs[:4]:
         c.wait()
+    def tiles_off(d):
+        return [
+            {"tile": lax.rem(t + d, n_tile)},
+            {"tile": lax.rem(t + n_tile - d, n_tile)},
+        ]
+
+    def greet(n, others):
+        for p in others:
+            pl.semaphore_signal(
+                hello.at[n], inc=1, device_id=p, device_id_type=MESH
+            )
+
     two = count[0] - 1
     two_f = two.astype(F32)
     one_f = 1.0 - two_f
@@ -292,6 +304,8 @@
     prep_t(0, (0, 2))
     forward_edges(ht, 0)
     pl.semaphore_wait(barrier, len(partners))
+    greet(0, tiles_off(1))
+    greet(1, beside)
     moved = start(exchange(0, xs.at[0, 0], xs.at[0, 1]))
     pending += moved
     sweep(fill_own)
@@ -300,6 +314,9 @@
     weights_here(1)
     prep_t(1, (0, 1, 2))
     landed(moved)
+    pl.semaphore_wait(hello.at[0], 2)
+    pl.semaphore_wait(hello.at[1], len(beside))
+    greet(2, tiles_off(2))
     before, after = from_sides(0)
     pre_one = own + before + after
     pre[...] = pre_one
@@ -315,6 +332,8 @@
         [cot[:B, :].astype(F32).T, cot[B:, :].astype(F32).T], axis=1
     )
     landed(moved)
+    pl.semaphore_wait(hello.at[2], 2)
+    greet(3, tiles_off(4))
     before, after = from_sides(1)
     total = own + before + after
     value, slope = silu_parts(total)
@@ -564,6 +583,8 @@
 
     back_own(1)
     landed(moved)
+    pl.semaphore_wait(hello.at[3], 2)
+    greet(4, tiles_off(8))
     back_edges(1, 2)
     grad_mid = nn(wc[1], gt[...])
     slope = silu_parts(pre[...])[1]
@@ -590,6 +611,7 @@
     for j in range(2):
         dx_ref[j * B : (j + 1) * B, :] = grad_in[:, j * B : (j + 1) * B].T.astype(BF)
     near_one = send_near(0, cross_one)
+    pl.semaphore_wait(hello.at[4], 2)
     far_two = send_far(1, near_two)
     far_one = send_far(0, near_one)
     last_two = send_last(1, far_two)
@@ -687,6 +709,7 @@
             dma((2, zside)),
             dma((2,)),
             dma((2,)),
+            pltpu.SemaphoreType.REGULAR((5,)),
         ],
         compiler_params=pltpu.CompilerParams(
             collective_id=0, has_side_effects=True, vmem_limit_bytes=48 * 1024 * 1024

time: 64.3 us -> 62.9 us (0.978)
  Pallas kernels: 62.8 us -> 61.5 us
    pallas_call x1, Pallas kernels: 62.1 us -> 60.7 us  [on_device(): pl.pallas_call(functools.partial(kernel, dims), out_shape=(jax.ShapeDtype...]
where the time goes in v5:
time: 62.9 us; the launch traced here: 62.8 us
  Pallas kernels  61.5 us (98%)
  between operations  1.29 us (2%)
    pallas_call x1, Pallas kernels, on_device(): pl.pallas_call(functools.partial(kernel, dims), out_shape=(jax.ShapeDtype...  60.7 us

profile of v5, /device:TPU:1, one launch (start us, length us, event | category | flops | bytes accessed | tf_op | source)
XLA Modules:
  0.0 62.8 jit_solution(7653921609020277809)
XLA Ops:
  1.3 60.7 %shard_map.102 = (bf16[256,128]{1,0:T(8,128)(2,1)S(1)}, bf16[256,128]{1,0:T(8,128)(2,1)S(1)}, f32[216,128]{1,0:T(8,128)S(1)}, f32[216,128]{1,0:T(8,128)S(1)}) custom-call(bf16[256,128]{1,0:T(8,128)(2,1)} %feat_hbm.1, s32[27,2,128]{2,1,0:T(2,128)} %src_hbm.1, s32[2,27]{1,0:T(2,128)} %bitcast.1, s32[1]{0:T(128)S(6)} %copy.11.count_hbm, ...), custom_call_target="tpu_custom_call" | custom-call | tf_op jit(solution)/shard_map/pallas_call | solution.py:653
  62.0 0.8 %shard_map.103 = (bf16[256,128]{1,0:T(8,128)(2,1)}, bf16[256,128]{1,0:T(8,128)(2,1)}, f32[216,128]{1,0:T(8,128)}, f32[216,128]{1,0:T(8,128)}) custom-call(bf16[256,128]{1,0:T(8,128)(2,1)S(1)} %get-tuple-element.8.refs_0_, bf16[256,128]{1,0:T(8,128)(2,1)S(1)} %get-tuple-element.9.refs_1_, f32[216,128]{1,0:T(8,128)S(1)} %get-tuple-element.10.refs_2_, ...), custom_call_target="tpu_custom_call" | custom-call | tf_op jit(solution)/shard_map/pallas_call | solution.py:726

commit v6 on v5

--- a/solution.py
+++ b/solution.py
@@ -547,7 +547,7 @@
                     device_id={"tile": far_z(d)},
                     device_id_type=MESH,
                 )
-                for d in range(1, zside)
+                for d in (2, 1, 3)
             ]
         )
 
@@ -582,16 +582,18 @@
         wgf[w, kvol * B :, :] = jnp.zeros((wgf.shape[1] - kvol * B, B), F32)
 
     back_own(1)
+    grad_mid = nn(wc[1, :, :n1], gt[:n1, :])
+    weight_grads(hid, 1, (1,))
     landed(moved)
     pl.semaphore_wait(hello.at[3], 2)
     greet(4, tiles_off(8))
     back_edges(1, 2)
-    grad_mid = nn(wc[1], gt[...])
+    grad_mid = grad_mid + nn(wc[1, :, n1:], gt[n1:, :])
     slope = silu_parts(pre[...])[1]
     q[0] = (grad_mid * slope * mask).astype(BF)
     moved = start(exchange(3, q.at[0], q.at[0]))
     pending += moved
-    weight_grads(hid, 1, (0, 1, 2))
+    weight_grads(hid, 1, (0, 2))
     pair_two = send_pair(1)
     back_own(0)
     weight_grads(ht, 0, (1,))
@@ -615,8 +617,8 @@
     far_two = send_far(1, near_two)
     far_one = send_far(0, near_one)
     last_two = send_last(1, far_two)
+    last_one = send_last(0, far_one)
     finish(1, last_two)
-    last_one = send_last(0, far_one)
     finish(0, last_one)
     for w in (pair_two, first_two, second_two, third_two, cross_two, near_two):
         pending += w

time: 62.9 us -> 62.8 us (level)
  no operation moved by 1% of the time
where the time goes in v6:
time: 62.8 us; the launch traced here: 62.6 us
  Pallas kernels  61.4 us (98%)
  between operations  1.29 us (2%)
    pallas_call x1, Pallas kernels, on_device(): pl.pallas_call(functools.partial(kernel, dims), out_shape=(jax.ShapeDtype...  60.6 us

profile of v6, /device:TPU:1, one launch (start us, length us, event | category | flops | bytes accessed | tf_op | source)
XLA Modules:
  0.0 62.6 jit_solution(16050573800409704571)
XLA Ops:
  1.3 60.6 %shard_map.102 = (bf16[256,128]{1,0:T(8,128)(2,1)S(1)}, bf16[256,128]{1,0:T(8,128)(2,1)S(1)}, f32[216,128]{1,0:T(8,128)S(1)}, f32[216,128]{1,0:T(8,128)S(1)}) custom-call(bf16[256,128]{1,0:T(8,128)(2,1)} %feat_hbm.1, s32[27,2,128]{2,1,0:T(2,128)} %src_hbm.1, s32[2,27]{1,0:T(2,128)} %bitcast.1, s32[1]{0:T(128)S(6)} %copy.11.count_hbm, ...), custom_call_target="tpu_custom_call" | custom-call | tf_op jit(solution)/shard_map/pallas_call | solution.py:655
  61.9 0.8 %shard_map.103 = (bf16[256,128]{1,0:T(8,128)(2,1)}, bf16[256,128]{1,0:T(8,128)(2,1)}, f32[216,128]{1,0:T(8,128)}, f32[216,128]{1,0:T(8,128)}) custom-call(bf16[256,128]{1,0:T(8,128)(2,1)S(1)} %get-tuple-element.8.refs_0_, bf16[256,128]{1,0:T(8,128)(2,1)S(1)} %get-tuple-element.9.refs_1_, f32[216,128]{1,0:T(8,128)S(1)} %get-tuple-element.10.refs_2_, ...), custom_call_target="tpu_custom_call" | custom-call | tf_op jit(solution)/shard_map/pallas_call | solution.py:728

commit v7 on v6

--- a/solution.py
+++ b/solution.py
@@ -604,8 +604,8 @@
     pair_one = send_pair(0)
     third_two = ring_close(1, first_two)
     first_one, second_one = ring_open(0, pair_one)
+    third_one = ring_close(0, first_one)
     cross_two = cross(1, pair_two, second_two, third_two)
-    third_one = ring_close(0, first_one)
     prep_c(0)
     grad_in = nn(wc[0], gt[...]) + q[1].astype(F32)
     cross_one = cross(0, pair_one, second_one, third_one)

time: 62.8 us -> 63 us (level)
  no operation moved by 1% of the time
where the time goes in v7:
time: 63 us; the launch traced here: 62.9 us
  Pallas kernels  61.6 us (98%)
  between operations  1.29 us (2%)
    pallas_call x1, Pallas kernels, on_device(): pl.pallas_call(functools.partial(kernel, dims), out_shape=(jax.ShapeDtype...  60.8 us

profile of v7, /device:TPU:1, one launch (start us, length us, event | category | flops | bytes accessed | tf_op | source)
XLA Modules:
  0.0 62.9 jit_solution(4418380781182761141)
XLA Ops:
  1.3 60.8 %shard_map.102 = (bf16[256,128]{1,0:T(8,128)(2,1)S(1)}, bf16[256,128]{1,0:T(8,128)(2,1)S(1)}, f32[216,128]{1,0:T(8,128)S(1)}, f32[216,128]{1,0:T(8,128)S(1)}) custom-call(bf16[256,128]{1,0:T(8,128)(2,1)} %feat_hbm.1, s32[27,2,128]{2,1,0:T(2,128)} %src_hbm.1, s32[2,27]{1,0:T(2,128)} %bitcast.1, s32[1]{0:T(128)S(6)} %copy.11.count_hbm, ...), custom_call_target="tpu_custom_call" | custom-call | tf_op jit(solution)/shard_map/pallas_call | solution.py:655
  62.1 0.8 %shard_map.103 = (bf16[256,128]{1,0:T(8,128)(2,1)}, bf16[256,128]{1,0:T(8,128)(2,1)}, f32[216,128]{1,0:T(8,128)}, f32[216,128]{1,0:T(8,128)}) custom-call(bf16[256,128]{1,0:T(8,128)(2,1)S(1)} %get-tuple-element.8.refs_0_, bf16[256,128]{1,0:T(8,128)(2,1)S(1)} %get-tuple-element.9.refs_1_, f32[216,128]{1,0:T(8,128)S(1)} %get-tuple-element.10.refs_2_, ...), custom_call_target="tpu_custom_call" | custom-call | tf_op jit(solution)/shard_map/pallas_call | solution.py:728
